TPU v7x, 128 devices: a whole 4x4x4 slice. The times are simulated.
128 devices in a mesh: dp: 16 (over y, x), chan: 8 (over z, core).
Axes of the slice: x: 4, y: 4, z: 4, core: 2. Of those that a mesh axis runs over, the one named last changes fastest.
Arguments:
- signal: bfloat16 [16, 512, 8192], P('dp', 'chan'), may hold values from -6 to 6
- signal_grad: bfloat16 [16, 512, 8192], P('dp', 'chan'), may hold values from -6 to 6
- embed_weight: float32 [64, 33], replicated, may hold values from -1 to 1
- embed_bias: float32 [64], replicated, may hold values from -3.140625 to 3.140625
- hidden_weight: float32 [64, 64], replicated, may hold values from -0.75 to 0.75
- frequency: float32 [2, 64], replicated, may hold values from 0.5 to 2
- output_weight: float32 [512, 64], replicated, may hold values from -0.75 to 0.75
- decay_rate: float32 [512], replicated, may hold values from 0.3 to 30
Outputs:
- filter_grad: float32 [512, 16384], P(None, ('dp', 'chan'))
- embed_grad: float32 [64, 33], replicated
- bias_grad: float32 [64], replicated
- hidden_grad: float32 [64, 64], replicated
- frequency_grad: float32 [2, 64], replicated
- output_grad: float32 [512, 64], replicated
- decay_grad: float32 [512], replicated
All inputs are finite; a program needn't handle non-finite values.
Results may differ from a plain program's by a relative error of at most 0.0003.
Values may be sent and summed in bfloat16 or wider, within the bound.
A program may use at most 64 MiB of HBM per device.

v0:
```python
import math

import jax
import jax.numpy as jnp
from jax import lax
from jax.sharding import Mesh
from jax.sharding import PartitionSpec as P

DP = ("dp_0", "dp_1")
DP_CHAN = ("dp_0", "dp_1", "chan_0", "chan_1")
CHAN = ("chan_0", "chan_1")


def side_by_side(arrays, axis, dim, along):
    ends, at = ([], 0)
    for a in arrays[:-1]:
        at += a.shape[along]
        ends.append(at)
    both = jnp.concatenate(arrays, axis=along)
    return tuple(
        jnp.split(lax.psum_scatter(both, axis, scatter_dimension=dim, tiled=True), ends, axis=along)
    )


def split_up(x, dim, peers):
    shape = x.shape
    blocks = x.reshape(*shape[:dim], peers, shape[dim] // peers, *shape[dim + 1 :])
    return jnp.moveaxis(blocks, dim, 0)


def laid_out(blocks, dim):
    shape = list(blocks.shape[1:])
    shape[dim] *= blocks.shape[0]
    return jnp.moveaxis(blocks, 0, dim).reshape(shape)


def joined_exchange(x, axis, axes, splits, concats):
    sizes = [lax.axis_size(a) for a in axes]
    blocks = split_up(x, splits[0], sizes[0])
    blocks = jnp.moveaxis(split_up(blocks, splits[1] + 1, sizes[1]), 0, 1)
    inside = blocks.shape[2:]
    blocks = blocks.reshape(-1, *inside)
    blocks = lax.all_to_all(blocks, axis, split_axis=0, concat_axis=0, tiled=True)
    blocks = laid_out(blocks.reshape(*sizes, *inside), concats[0] + 1)
    return laid_out(blocks, concats[1])


def sum_at_owner(x, axis, dim):
    blocks = split_up(x, dim, lax.axis_size(axis))
    arrived = lax.all_to_all(blocks, axis, split_axis=0, concat_axis=0, tiled=True)
    return arrived.sum(axis=0)


def summed_rows(x, axes, dim):
    far, near = axes
    blocks = split_up(x, dim, lax.axis_size(far))
    nearer = sum_at_owner(blocks, near, dim + 1)
    arrived = lax.all_to_all(nearer, far, split_axis=0, concat_axis=0, tiled=True)
    return arrived.sum(axis=0)


def filled_up(lines, peers):
    spare = -len(lines) % peers
    return jnp.pad(lines, [(0, spare)] + [(0, 0)] * (lines.ndim - 1))


def copy_for_each(x, axis):
    peers = lax.axis_size(axis)
    return lax.all_to_all(jnp.broadcast_to(x[None], (peers, *x.shape)), axis, 0, 0, tiled=True)


def gathered_by_axis(x, axes, dim):
    far, near = axes
    blocks = copy_for_each(copy_for_each(x, far), near)
    return laid_out(blocks.swapaxes(0, 1).reshape(-1, *x.shape), dim)


def total_of(x, axes):
    own = summed_rows(filled_up(x, lax.axis_size(axes[0]) * lax.axis_size(axes[1])), axes, 0)
    whole = gathered_by_axis(own, axes, 0)
    return whole[: len(x)].reshape(x.shape)


def together(arrays, axis):
    vector, at, finished = (jnp.concatenate([a.reshape(-1) for a in arrays]), 0, [])
    running = total_of(vector, axis)
    for a in arrays:
        finished.append(running[at : at + a.size].reshape(a.shape))
        at += a.size
    return tuple(finished)


def lag_features(lag, length, bands):
    total = 2 * length
    scaled = lag.astype(jnp.float32) / length
    sines = []
    cosines = []
    for band in range(bands):
        factor = max(1, int(0.45 * total * 10000.0 ** (-band / bands)))
        phase = (lag * factor % total).astype(jnp.float32) * (2.0 * math.pi / total)
        sines.append(jnp.sin(phase))
        cosines.append(jnp.cos(phase))
    return jnp.stack([scaled] + sines + cosines)


def filter_loss(params, lag, cotangent, length):
    embed_weight, embed_bias, hidden_weight, frequency, output_weight, decay_rate = params
    bands = (embed_weight.shape[1] - 1) // 2
    exact = lax.Precision.HIGHEST
    table = lag_features(lag, length, bands)
    first = jnp.sin(
        frequency[0][:, None]
        * (
            jnp.dot(embed_weight, table, precision=exact, preferred_element_type=jnp.float32)
            + embed_bias[:, None]
        )
    )
    second = jnp.sin(
        frequency[1][:, None]
        * jnp.dot(hidden_weight, first, precision=exact, preferred_element_type=jnp.float32)
    )
    shaped = jnp.dot(output_weight, second, precision=exact, preferred_element_type=jnp.float32)
    window = jnp.exp(-decay_rate[:, None] * jnp.abs(lag).astype(jnp.float32)[None, :] / length)
    return jnp.sum(shaped * window * cotangent) / math.sqrt(2 * length)


def plan_sizes(total):
    bits = total.bit_length() - 1
    side = 2 ** min(7, bits // 2)
    return (total // (side * side), side, side)


def rotation(rows, cols, modulus, sign):
    row_index = jnp.arange(rows, dtype=jnp.int32)
    col_index = jnp.arange(cols, dtype=jnp.int32)
    product = row_index[:, None] * col_index[None, :] % modulus
    angle = product.astype(jnp.float32) * (-2.0 * math.pi / modulus)
    return (jnp.cos(angle), sign * jnp.sin(angle))


def twist(real_part, imag_part, table):
    cosine, sine = table
    return (real_part * cosine - imag_part * sine, real_part * sine + imag_part * cosine)


def table_product(spec, table, real_part, imag_part, table_first):
    cosine, sine = table
    exact = lax.Precision.HIGHEST

    def apply(matrix, values):
        if table_first:
            return jnp.einsum(
                spec, matrix, values, precision=exact, preferred_element_type=jnp.float32
            )
        return jnp.einsum(spec, values, matrix, precision=exact, preferred_element_type=jnp.float32)

    common = apply(cosine, real_part + imag_part)
    return (common - apply(cosine + sine, imag_part), common + apply(sine - cosine, real_part))


def forward(real_part, imag_part, total):
    outer, middle, inner = plan_sizes(total)
    leading = real_part.shape[:-1]
    real_part = real_part.reshape(leading + (outer, middle * inner))
    imag_part = imag_part.reshape(leading + (outer, middle * inner))
    real_part, imag_part = table_product(
        "kp,...pm->...km", rotation(outer, outer, outer, 1.0), real_part, imag_part, True
    )
    real_part, imag_part = twist(real_part, imag_part, rotation(outer, middle * inner, total, 1.0))
    real_part = real_part.reshape(leading + (outer, middle, inner))
    imag_part = imag_part.reshape(leading + (outer, middle, inner))
    real_part, imag_part = table_product(
        "aq,...kqr->...kar", rotation(middle, middle, middle, 1.0), real_part, imag_part, True
    )
    real_part, imag_part = twist(real_part, imag_part, rotation(middle, inner, middle * inner, 1.0))
    return table_product(
        "...kar,rb->...kab", rotation(inner, inner, inner, 1.0), real_part, imag_part, False
    )


def inverse(real_part, imag_part, total):
    outer, middle, inner = plan_sizes(total)
    leading = real_part.shape[:-3]
    exact = lax.Precision.HIGHEST
    real_part, imag_part = table_product(
        "...kab,rb->...kar", rotation(inner, inner, inner, -1.0), real_part, imag_part, False
    )
    real_part, imag_part = twist(
        real_part, imag_part, rotation(middle, inner, middle * inner, -1.0)
    )
    real_part, imag_part = table_product(
        "qa,...kar->...kqr", rotation(middle, middle, middle, -1.0), real_part, imag_part, True
    )
    real_part = real_part.reshape(leading + (outer, middle * inner))
    imag_part = imag_part.reshape(leading + (outer, middle * inner))
    real_part, imag_part = twist(real_part, imag_part, rotation(outer, middle * inner, total, -1.0))
    cosine, sine = rotation(outer, outer, outer, -1.0)
    result = jnp.einsum(
        "pk,...km->...pm", cosine, real_part, precision=exact, preferred_element_type=jnp.float32
    )
    result = result - jnp.einsum(
        "pk,...km->...pm", sine, imag_part, precision=exact, preferred_element_type=jnp.float32
    )
    return result.reshape(leading + (total,)) / total


def mirror(values):
    flipped = jnp.flip(values, (-3, -2, -1))
    shifted = jnp.roll(flipped, 1, axis=-3)
    head = jnp.roll(shifted[..., 0, :, :], 1, axis=-2)
    first_row = (jnp.arange(head.shape[-2]) == 0)[:, None]
    head = jnp.where(first_row, jnp.roll(head, 1, axis=-1), head)
    return jnp.concatenate([head[..., None, :, :], shifted[..., 1:, :, :]], axis=-3)


def block_spectrum(inputs, grads, total):
    padding = jnp.zeros(inputs.shape[:-1] + (total - inputs.shape[-1],), jnp.float32)
    real_part = jnp.concatenate([inputs.astype(jnp.float32), padding], axis=-1)
    imag_part = jnp.concatenate([grads.astype(jnp.float32), padding], axis=-1)
    spectrum_real, spectrum_imag = forward(real_part, imag_part, total)
    back_real = mirror(spectrum_real)
    back_imag = -mirror(spectrum_imag)
    in_real = 0.5 * (spectrum_real + back_real)
    in_imag = 0.5 * (spectrum_imag + back_imag)
    grad_real = 0.5 * (spectrum_imag - back_imag)
    grad_imag = -0.5 * (spectrum_real - back_real)
    cross_real = in_real * grad_real + in_imag * grad_imag
    cross_imag = in_real * grad_imag - in_imag * grad_real
    return (jnp.sum(cross_real, axis=0), jnp.sum(cross_imag, axis=0))


def corner_mask(outer, middle, width):
    first_k = jnp.arange(outer, dtype=jnp.int32)[:, None, None] == 0
    first_a = jnp.arange(middle, dtype=jnp.int32)[None, :, None] == 0
    first_b = jnp.arange(width, dtype=jnp.int32)[None, None, :] == 0
    return first_k & first_a & first_b


def fold_half(cross_real, cross_imag):
    outer, middle, inner = cross_real.shape[-3:]
    half = inner // 2
    corner = corner_mask(outer, middle, half)
    send_real = cross_real[..., :half]
    send_imag = jnp.where(corner, cross_real[..., half : half + 1], cross_imag[..., :half])
    return (send_real, send_imag)


def unfold_half(half_real, half_imag):
    outer, middle, half = half_real.shape[-3:]
    corner = corner_mask(outer, middle, half)
    low_real = jnp.where(corner, 0.5 * half_real, half_real)
    low_imag = jnp.where(corner, 0.0, half_imag)
    top = 0.5 * half_imag[..., :1, :1, :1]
    high_real = jnp.where(corner, top, 0.0)
    high_imag = jnp.zeros_like(half_imag)
    whole_real = jnp.concatenate([low_real, high_real], axis=-1)
    whole_imag = jnp.concatenate([low_imag, high_imag], axis=-1)
    return (whole_real + mirror(whole_real), whole_imag - mirror(whole_imag))


def local(
    signal,
    signal_grad,
    embed_weight,
    embed_bias,
    hidden_weight,
    frequency,
    output_weight,
    decay_rate,
):
    seq_local, chan_local, length = signal.shape
    total = 2 * length
    block = 8
    scale = 1.0 / math.sqrt(seq_local * lax.axis_size(DP) * length)
    indices = jnp.arange(chan_local // block, dtype=jnp.int32)

    def spectrum_of(index):
        start = index * block
        inputs = lax.dynamic_slice_in_dim(signal, start, block, 1)
        grads = lax.dynamic_slice_in_dim(signal_grad, start, block, 1)
        return block_spectrum(inputs, grads, total)

    def half_of(index):
        cross_real, cross_imag = spectrum_of(index)
        return fold_half(cross_real, cross_imag)

    half_real, half_imag = lax.map(half_of, indices)
    tail = half_real.shape[2:]
    half_real = half_real.reshape((chan_local,) + tail) * scale
    half_imag = half_imag.reshape((chan_local,) + tail) * scale
    own_real, own_imag = side_by_side((half_real, half_imag), DP, 0, 1)
    full_real, full_imag = unfold_half(own_real, own_imag)
    own_lags = inverse(full_real, full_imag, total)
    filter_grad = joined_exchange(own_lags, DP_CHAN, (DP, CHAN), (1, 1), (0, 0))
    lag_count = filter_grad.shape[1]
    device_rank = lax.axis_index(DP) * lax.axis_size(CHAN) + lax.axis_index(CHAN)
    position = device_rank * lag_count + jnp.arange(lag_count, dtype=jnp.int32)
    lag = jnp.where(position < length, position, position - total)
    params = (embed_weight, embed_bias, hidden_weight, frequency, output_weight, decay_rate)
    local_grads = jax.grad(filter_loss)(params, lag, filter_grad, length)
    summed = together(
        (
            local_grads[0],
            local_grads[1],
            local_grads[2],
            local_grads[3],
            local_grads[4],
            local_grads[5],
        ),
        (("dp_0", "dp_1", "chan_0"), "chan_1"),
    )
    return (filter_grad, summed[0], summed[1], summed[2], summed[3], summed[4], summed[5])


def solution(mesh):
    torus = Mesh(mesh.devices.reshape(4, 4, 4, 2), ("dp_0", "dp_1", "chan_0", "chan_1"))
    return jax.shard_map(
        local,
        mesh=torus,
        in_specs=(P(DP, CHAN, None), P(DP, CHAN, None), P(), P(), P(), P(), P(), P()),
        out_specs=(P(None, DP_CHAN), P(), P(), P(), P(), P(), P()),
        check_vma=False,
    )
```

profile of v0, /device:TPU:1, one launch (start us, length us, event | category | flops | bytes accessed | tf_op | source)
XLA Modules:
  0.0 305.3 jit_solution(15409766969200912248)
XLA Ops:
  7.3 130.8 %while.15 = (s32[]{:T(128)}, f32[8,8,1,128,64]{3,4,1,2,0:T(8,128)}, f32[8,8,1,128,64]{3,4,1,2,0:T(8,128)}, s32[8]{0:T(128)S(1)}, bf16[1,64,8192]{2,1,0:T(8,128)(...) while((s32[]{:T(128)}, f32[8,8,1,128,64]{3,4,1,2,0:T(8,128)}, ...), condition=%wide.region_1.2_spmd, body=%wide.region_0.1_spmd.sunk | while | flops 1217667328 | bytes 33846496 | solution.py:287
  14.0 1.0 fusion.338
  17.6 1.0 fusion.343
  30.3 1.0 fusion.338
  33.9 1.0 fusion.343
  46.7 1.0 fusion.338
  50.3 1.0 fusion.343
  66.6 1.0 fusion.343
  79.4 1.0 fusion.338
  83.0 1.0 fusion.343
  95.7 1.0 fusion.338
  99.3 1.0 fusion.343
  112.1 1.0 fusion.338
  115.7 1.0 fusion.343
  132.0 1.0 fusion.343
  138.0 2.7 broadcast_multiply_fusion
  140.7 2.2 pad_maximum_fusion.2
  144.9 77.3 %reduce-scatter.2.cloned.1.call-done = f32[4,2,128,64]{2,3,1,0:T(8,128)} async-done(((f32[64,2,128,64]{2,3,1,0:T(8,128)}), f32[4,2,128,64]{2,3,1,0:T(8,128)}) %reduce-scatter.2.cloned.1.call-update) | async-done | bytes 262160 | tf_op jit(solution)/shard_map/reduce_scatter | solution.py:21
  231.6 9.3 %all-to-all-start = ((f32[128,4,128]{2,1,0:T(4,128)}), f32[128,4,128]{2,1,0:T(4,128)S(1)}, u32[]{:S(2)}, u32[]{:S(2)}) async-start(f32[128,4,128]{2,1,0:T(4,128)} %bitcast.70), calls=%async_computation.1 | async-start | bytes 524288 | tf_op jit(solution)/shard_map/all_to_all | solution.py:43
  241.3 10.5 %all-to-all-done = f32[128,4,128]{2,1,0:T(4,128)S(1)} async-done(((f32[128,4,128]{2,1,0:T(4,128)}), f32[128,4,128]{2,1,0:T(4,128)S(1)}, u32[]{:S(2)}, u32[]{:S(2)}) %all-to-all-start) | async-done | bytes 262176 | tf_op jit(solution)/shard_map/all_to_all | solution.py:43
  256.0 4.6 %all_to_all.30 = f32[2,64,310]{2,1,0:T(8,128)S(1)} all-to-all(f32[2,64,310]{2,1,0:T(8,128)S(1)} %copy.360), channel_id=1, replica_groups=mesh['dp_0'=4,'dp_1'=4,'chan_0'=4,'chan_1'=2] {'chan_1'}, dimensions={0} | all-to-all | bytes 317440 | tf_op jit(solution)/shard_map/all_to_all | solution.py:50
  260.7 13.0 %all_to_all.31 = f32[64,1,310]{2,1,0:T(1,128)S(1)} all-to-all(f32[64,1,310]{2,1,0:T(1,128)S(1)} %all_to_all.21), channel_id=1, replica_groups=mesh['dp_0'=4,'dp_1'=4,'chan_0'=4,'chan_1'=2] {'dp_0','dp_1','chan_0'}, dimensions={0} | all-to-all | bytes 158720 | tf_op jit(solution)/shard_map/all_to_all | solution.py:58
  273.8 13.4 %all_to_all.32 = f32[64,1,310]{2,1,0:T(1,128)S(1)} all-to-all(f32[64,1,310]{2,1,0:T(1,128)S(1)} %broadcast_in_dim.182), channel_id=1, replica_groups=mesh['dp_0'=4,'dp_1'=4,'chan_0'=4,'chan_1'=2] {'dp_0','dp_1','chan_0'}, dimensions={0} | all-to-all | bytes 158720 | tf_op jit(solution)/shard_map/all_to_all | solution.py:69
  287.2 6.4 %all_to_all.33 = f32[2,64,310]{2,1,0:T(8,128)S(1)} all-to-all(f32[2,64,310]{2,1,0:T(8,128)S(1)} %broadcast_in_dim.184), channel_id=1, replica_groups=mesh['dp_0'=4,'dp_1'=4,'chan_0'=4,'chan_1'=2] {'chan_1'}, dimensions={0} | all-to-all | bytes 317440 | tf_op jit(solution)/shard_map/all_to_all | solution.py:69
  (379 shorter events, 130.7 us)
Async XLA Ops:
  7.2 245.7 %copy-start = (f32[512,64]{0,1:T(8,128)S(1)}, f32[512,64]{0,1:T(8,128)}, u32[]{:S(2)}) copy-start(f32[512,64]{0,1:T(8,128)} %param.16) | copy-start | bytes 393220
  7.2 215.0 %reduce-scatter.2.cloned.1.call-start = ((), (), s32[]{:S(2)}) async-start(), calls=%async_computation.6 | async-start | bytes 4456448 | tf_op jit(solution)/shard_map/reduce_scatter | solution.py:21
  20.7 1.0 copy-start.1
  20.7 1.2 copy-start.2
  37.1 1.0 copy-start.1
  37.1 1.2 copy-start.2
  53.4 1.0 copy-start.1
  53.4 1.2 copy-start.2
  69.7 1.0 copy-start.1
  69.7 1.2 copy-start.2
  86.1 1.0 copy-start.1
  86.1 1.2 copy-start.2
  102.4 1.2 copy-start.2
  118.8 1.2 copy-start.2
  135.1 1.0 copy-start.1
  135.1 1.2 copy-start.2
  143.0 1.6 copy-start.7
  143.0 1.7 copy-start.8
  143.0 1.7 copy-start.9
  222.2 1.8 copy-start.4
  229.6 11.3 %copy-start.6 = (f32[512]{0:T(512)S(1)}, f32[512]{0:T(512)}, u32[]{:S(2)}) copy-start(f32[512]{0:T(512)} %param.17) | copy-start | bytes 6148
  229.6 11.3 %copy-start.5 = (f32[64,64]{1,0:T(8,128)S(1)}, f32[64,64]{1,0:T(8,128)}, u32[]{:S(2)}) copy-start(f32[64,64]{1,0:T(8,128)} %param.14) | copy-start | bytes 49156
  231.6 20.2 %all-to-all-start = ((f32[128,4,128]{2,1,0:T(4,128)}), f32[128,4,128]{2,1,0:T(4,128)S(1)}, u32[]{:S(2)}, u32[]{:S(2)}) async-start(f32[128,4,128]{2,1,0:T(4,128)} %bitcast.70), calls=%async_computation.1 | async-start | bytes 524288 | tf_op jit(solution)/shard_map/all_to_all | solution.py:43
  252.0 4.0 %copy-start.3 = (f32[8,16,4,128]{3,2,1,0:T(4,128)}, f32[8,16,4,128]{3,2,1,0:T(4,128)S(1)}, u32[]{:S(2)}) copy-start(f32[8,16,4,128]{3,2,1,0:T(4,128)S(1)} %copy.356) | copy-start | bytes 786436
  (2 other events, 2.1 us)
Sparse Core Ops, SparseCore 0:
  143.1 79.0 reduce-scatter.1
where the time goes:
time: 306 us; the launch traced here: 305 us
  waiting for transfers between devices  87.8 us (29%)
  local copies, waits for them, and re-layouts  66.4 us (22%)
  matrix products  51.6 us (17%)
  blocking collectives  37.4 us (12%)
  other arithmetic  31.6 us (10%)
  between operations  14.6 us (5%)
  starting transfers between devices  9.37 us (3%)
  loops' own time  6.51 us (2%)
    reduce_scatter x1, waiting for transfers between devices, side_by_side(): lax.psum_scatter(both, axis, scatter_dimension=dim, tiled=True)  77.3 us
    dot_general x27, matrix products, apply(): jnp.einsum(spec, values, matrix, precision=exact, preferred_element_type=...  25.7 us
    dot_general x27, matrix products, apply(): jnp.einsum(spec, matrix, values, precision=exact, preferred_element_type=...  22.3 us
    all_to_all x2, blocking collectives, copy_for_each(): lax.all_to_all(jnp.broadcast_to(x[None], (peers, *x.shape)), axis, 0, 0,...  19.8 us
    slice x32, local copies, waits for them, and re-layouts, mirror(): head = jnp.roll(shifted[..., 0, :, :], 1, axis=-2)  18 us
    all_to_all x1, blocking collectives, summed_rows(): lax.all_to_all(nearer, far, split_axis=0, concat_axis=0, tiled=True)  13 us
    another operation x16, local copies, waits for them, and re-layouts  11.4 us
    all_to_all x1, waiting for transfers between devices, joined_exchange(): lax.all_to_all(blocks, axis, split_axis=0, concat_axis=0, tiled=True)  10.5 us
  transfers between devices with their start and end apart: 2, of which 2 were waited for; matrix products, arithmetic and copies ran while one was open for 1% of the time, Pallas kernels for 0%

commit v1 on v0

v1 whole, which is shorter than its diff:
```python
import math

import jax
import jax.numpy as jnp
import numpy as np
from jax import lax
from jax.experimental import pallas as pl
from jax.experimental.pallas import tpu as pltpu
from jax.sharding import Mesh
from jax.sharding import PartitionSpec as P

DP = ("y", "x")
CHAN = ("z", "core")
MESH_ID = pl.DeviceIdType.MESH
OFFSETS = sorted(
    [(dy, dx) for dy in range(4) for dx in range(4)],
    key=lambda p: (min(p[0], 4 - p[0]) + min(p[1], 4 - p[1])),
)
PEERS = [(dz, dc) for dz in range(4) for dc in range(2)]


def split_table(values):
    high = values.astype(jnp.bfloat16)
    low = (values - high.astype(np.float64)).astype(jnp.bfloat16)
    return high, low


def transform_tables(total, scale):
    half, side = 64, 128
    k1 = np.arange(half)[:, None] + 0.5
    n1 = np.arange(half)[None, :]
    angle = -2.0 * np.pi * k1 * n1 / side
    first = np.concatenate([np.cos(angle), np.sin(angle)], axis=0)
    first = np.concatenate(split_table(first), axis=1)
    n2 = np.arange(side)[None, :]
    angle = -2.0 * np.pi * k1 * n2 / total
    twist = np.stack([np.cos(angle), np.sin(angle)]).astype(np.float32)
    rows = np.arange(side)[:, None]
    angle = -2.0 * np.pi * (rows * n2 % side) / side
    cosine, sine = np.cos(angle), np.sin(angle)
    forward = np.block([[cosine, sine], [-sine, cosine]])
    high, low = split_table(forward)
    forward = np.concatenate([high, high, low], axis=0)
    backward = np.block([[cosine, -sine], [sine, cosine]])
    high, low = split_table(backward)
    backward = np.concatenate([high, high, low], axis=0)
    lag_row = np.arange(side)[:, None]
    freq = np.arange(half)[None, :] + 0.5
    angle = 2.0 * np.pi * lag_row * freq / side
    last = np.concatenate([np.cos(angle), -np.sin(angle)], axis=1)
    last = last * np.where(lag_row < half, 1.0, -1.0) * (2.0 * scale / total)
    high, low = split_table(last)
    last = np.concatenate([high, high, low], axis=1)
    return first, twist, forward, backward, last


def split_values(values):
    high = values.astype(jnp.bfloat16)
    low = (values - high.astype(jnp.float32)).astype(jnp.bfloat16)
    return high, low


def dot(a, b):
    return jnp.dot(a, b, preferred_element_type=jnp.float32)


def correlate_kernel(
    both,
    first,
    twist,
    forward,
    backward,
    last,
    out,
    arrived,
    spectrum,
    lags,
    mine,
    rows,
    landed,
    local_sem,
    send_sem,
    recv_sem,
    send2_sem,
    recv2_sem,
    send3_sem,
    recv3_sem,
):
    y, x = lax.axis_index("y"), lax.axis_index("x")
    z, core = lax.axis_index("z"), lax.axis_index("core")
    me = y * 4 + x
    group = z * 2 + core

    barrier = pltpu.get_barrier_semaphore()
    dp_peers = []
    for dy, dx in OFFSETS[1:]:
        ty, tx = lax.rem(y + dy, 4), lax.rem(x + dx, 4)
        dp_peers.append((ty * 4 + tx, {"y": ty, "x": tx}))
    chan_peers = []
    for dz, dc in PEERS[1:]:
        tz, tc = lax.rem(z + dz, 4), lax.rem(core + dc, 2)
        chan_peers.append((tz * 2 + tc, {"z": tz, "core": tc}))
    for _, where in dp_peers + chan_peers:
        pl.semaphore_signal(barrier, 1, device_id=where, device_id_type=MESH_ID)
    own = pltpu.make_async_copy(both.at[me], arrived.at[0], local_sem)
    own.start()
    spectrum[...] = jnp.zeros_like(spectrum)
    pl.semaphore_wait(barrier, len(dp_peers) + len(chan_peers))

    copies = []
    for at, (index, where) in enumerate(dp_peers):
        copy = pltpu.make_async_remote_copy(
            both.at[index],
            arrived.at[at + 1],
            send_sem.at[at],
            recv_sem.at[at],
            device_id=where,
            device_id_type=MESH_ID,
        )
        copy.start()
        copies.append(copy)

    cos_t, sin_t = twist[0], twist[1]

    def add_sequence(slot):
        parts = []
        for part in range(2):
            for channel in range(4):
                data = arrived[slot, channel, part]
                data = jnp.concatenate([data, data], axis=0)
                step = dot(first[...], data)
                real, imag = step[:64], step[64:]
                parts.append(
                    jnp.concatenate(
                        [real * cos_t - imag * sin_t, real * sin_t + imag * cos_t], axis=1
                    )
                )
        high, low = split_values(jnp.concatenate(parts, axis=0))
        whole = dot(jnp.concatenate([high, low, high], axis=1), forward[...])
        in_real, in_imag = whole[:256, :128], whole[:256, 128:]
        grad_real, grad_imag = whole[256:, :128], whole[256:, 128:]
        spectrum[:, :128] += in_real * grad_real + in_imag * grad_imag
        spectrum[:, 128:] += in_real * grad_imag - in_imag * grad_real

    own.wait()
    add_sequence(0)

    @pl.loop(0, 15)
    def _(at):
        pltpu.make_async_remote_copy(
            both.at[0],
            arrived.at[at + 1],
            send_sem.at[at],
            recv_sem.at[at],
            device_id={"y": y, "x": lax.rem(x + 1, 4)},
            device_id_type=MESH_ID,
        ).wait_recv()
        add_sequence(at + 1)

    high, low = split_values(spectrum[...])
    back = dot(jnp.concatenate([high, low, high], axis=1), backward[...])
    columns = []
    for channel in range(4):
        real = back[64 * channel : 64 * channel + 64, :128]
        imag = back[64 * channel : 64 * channel + 64, 128:]
        columns.append(
            jnp.concatenate([real * cos_t + imag * sin_t, imag * cos_t - real * sin_t], axis=0)
        )
    high, low = split_values(jnp.concatenate(columns, axis=1))
    result = dot(last[...], jnp.concatenate([high, low, high], axis=0))
    lags[...] = result.reshape(16, 8, 512)

    for copy in copies:
        copy.wait_send()

    copies = []
    for at, (index, where) in enumerate(dp_peers):
        copy = pltpu.make_async_remote_copy(
            lags.at[index],
            mine.at[me],
            send2_sem.at[at],
            recv2_sem.at[at],
            device_id=where,
            device_id_type=MESH_ID,
        )
        copy.start()
        copies.append(copy)
    mine[me] = lags[me]
    for copy in copies:
        copy.wait()

    for lag_row in range(8):
        for channel in range(4):
            rows[lag_row, pl.ds(channel, 16, stride=4), :] = mine[
                :, lag_row, 128 * channel : 128 * channel + 128
            ]

    copies = []
    for at, (index, where) in enumerate(chan_peers):
        copy = pltpu.make_async_remote_copy(
            rows.at[index],
            landed.at[group],
            send3_sem.at[at],
            recv3_sem.at[at],
            device_id=where,
            device_id_type=MESH_ID,
        )
        copy.start()
        copies.append(copy)
    landed[group] = rows[group]
    for copy in copies:
        copy.wait()
    out[...] = landed[...].reshape(512, 128)


def correlate(signal, signal_grad, total, scale):
    both = jnp.stack(
        [signal.reshape(16, 4, 64, 128), signal_grad.reshape(16, 4, 64, 128)], axis=2
    )
    tables = transform_tables(total, scale)
    vmem = pl.BlockSpec(memory_space=pltpu.VMEM)
    return pl.pallas_call(
        correlate_kernel,
        out_shape=jax.ShapeDtypeStruct((512, 128), jnp.float32),
        in_specs=[pl.BlockSpec(memory_space=pl.ANY)] + [vmem] * 5,
        out_specs=vmem,
        scratch_shapes=[
            pltpu.VMEM((16, 4, 2, 64, 128), jnp.bfloat16),
            pltpu.VMEM((256, 256), jnp.float32),
            pltpu.VMEM((16, 8, 512), jnp.float32),
            pltpu.VMEM((16, 8, 512), jnp.float32),
            pltpu.VMEM((8, 64, 128), jnp.float32),
            pltpu.VMEM((8, 64, 128), jnp.float32),
            pltpu.SemaphoreType.DMA,
            pltpu.SemaphoreType.DMA((15,)),
            pltpu.SemaphoreType.DMA((15,)),
            pltpu.SemaphoreType.DMA((15,)),
            pltpu.SemaphoreType.DMA((15,)),
            pltpu.SemaphoreType.DMA((7,)),
            pltpu.SemaphoreType.DMA((7,)),
        ],
        compiler_params=pltpu.CompilerParams(
            collective_id=0, has_side_effects=True, vmem_limit_bytes=32 * 1024 * 1024
        ),
    )(both, *[jnp.asarray(t) for t in tables])


def split_up(x, dim, peers):
    shape = x.shape
    blocks = x.reshape(*shape[:dim], peers, shape[dim] // peers, *shape[dim + 1 :])
    return jnp.moveaxis(blocks, dim, 0)


def laid_out(blocks, dim):
    shape = list(blocks.shape[1:])
    shape[dim] *= blocks.shape[0]
    return jnp.moveaxis(blocks, 0, dim).reshape(shape)


def sum_at_owner(x, axis, dim):
    blocks = split_up(x, dim, lax.axis_size(axis))
    arrived = lax.all_to_all(blocks, axis, split_axis=0, concat_axis=0, tiled=True)
    return arrived.sum(axis=0)


def summed_rows(x, axes, dim):
    far, near = axes
    blocks = split_up(x, dim, lax.axis_size(far))
    nearer = sum_at_owner(blocks, near, dim + 1)
    arrived = lax.all_to_all(nearer, far, split_axis=0, concat_axis=0, tiled=True)
    return arrived.sum(axis=0)


def filled_up(lines, peers):
    spare = -len(lines) % peers
    return jnp.pad(lines, [(0, spare)] + [(0, 0)] * (lines.ndim - 1))


def copy_for_each(x, axis):
    peers = lax.axis_size(axis)
    return lax.all_to_all(jnp.broadcast_to(x[None], (peers, *x.shape)), axis, 0, 0, tiled=True)


def gathered_by_axis(x, axes, dim):
    far, near = axes
    blocks = copy_for_each(copy_for_each(x, far), near)
    return laid_out(blocks.swapaxes(0, 1).reshape(-1, *x.shape), dim)


def total_of(x, axes):
    own = summed_rows(filled_up(x, lax.axis_size(axes[0]) * lax.axis_size(axes[1])), axes, 0)
    whole = gathered_by_axis(own, axes, 0)
    return whole[: len(x)].reshape(x.shape)


def together(arrays, axis):
    vector, at, finished = (jnp.concatenate([a.reshape(-1) for a in arrays]), 0, [])
    running = total_of(vector, axis)
    for a in arrays:
        finished.append(running[at : at + a.size].reshape(a.shape))
        at += a.size
    return tuple(finished)


def lag_features(lag, length, bands):
    total = 2 * length
    scaled = lag.astype(jnp.float32) / length
    sines = []
    cosines = []
    for band in range(bands):
        factor = max(1, int(0.45 * total * 10000.0 ** (-band / bands)))
        phase = (lag * factor % total).astype(jnp.float32) * (2.0 * math.pi / total)
        sines.append(jnp.sin(phase))
        cosines.append(jnp.cos(phase))
    return jnp.stack([scaled] + sines + cosines)


def filter_loss(params, lag, cotangent, length):
    embed_weight, embed_bias, hidden_weight, frequency, output_weight, decay_rate = params
    bands = (embed_weight.shape[1] - 1) // 2
    exact = lax.Precision.HIGHEST
    table = lag_features(lag, length, bands)
    first = jnp.sin(
        frequency[0][:, None]
        * (
            jnp.dot(embed_weight, table, precision=exact, preferred_element_type=jnp.float32)
            + embed_bias[:, None]
        )
    )
    second = jnp.sin(
        frequency[1][:, None]
        * jnp.dot(hidden_weight, first, precision=exact, preferred_element_type=jnp.float32)
    )
    shaped = jnp.dot(output_weight, second, precision=exact, preferred_element_type=jnp.float32)
    window = jnp.exp(-decay_rate[:, None] * jnp.abs(lag).astype(jnp.float32)[None, :] / length)
    return jnp.sum(shaped * window * cotangent) / math.sqrt(2 * length)


def local(
    signal,
    signal_grad,
    embed_weight,
    embed_bias,
    hidden_weight,
    frequency,
    output_weight,
    decay_rate,
):
    _, _, length = signal.shape
    total = 2 * length
    scale = 1.0 / math.sqrt(16 * length)
    filter_grad = correlate(signal[0], signal_grad[0], total, scale)
    lag_count = filter_grad.shape[1]
    device_rank = lax.axis_index(DP) * lax.axis_size(CHAN) + lax.axis_index(CHAN)
    position = device_rank * lag_count + jnp.arange(lag_count, dtype=jnp.int32)
    lag = jnp.where(position < length, position, position - total)
    params = (embed_weight, embed_bias, hidden_weight, frequency, output_weight, decay_rate)
    grads = jax.grad(filter_loss)(params, lag, filter_grad, length)
    summed = together(grads, (("y", "x", "z"), "core"))
    return (filter_grad, *summed)


def solution(mesh):
    torus = Mesh(mesh.devices.reshape(4, 4, 4, 2), ("y", "x", "z", "core"))
    return jax.shard_map(
        local,
        mesh=torus,
        in_specs=(P(DP, CHAN, None), P(DP, CHAN, None), P(), P(), P(), P(), P(), P()),
        out_specs=(P(None, DP + CHAN), P(), P(), P(), P(), P(), P()),
        check_vma=False,
    )
```

time: 306 us -> 111 us (0.36)
  waiting for transfers between devices: 87.8 us -> 0 us
  local copies, waits for them, and re-layouts: 66.4 us -> 8.71 us
  Pallas kernels: 0 us -> 48.3 us
  matrix products: 51.6 us -> 4.09 us
  other arithmetic: 31.6 us -> 7.33 us
  between operations: 14.6 us -> 1.23 us
  starting transfers between devices: 9.37 us -> 0 us
  loops' own time: 6.51 us -> 0 us
  blocking collectives: 37.4 us -> 40.8 us
    reduce_scatter x1 -> x0, waiting for transfers between devices: 77.3 us -> none  [side_by_side(): lax.psum_scatter(both, axis, scatter_dimension=dim, tiled=True)]
    pallas_call x0 -> x1, Pallas kernels: none -> 48.3 us  [correlate(): pl.pallas_call(correlate_kernel, out_shape=jax.ShapeDtypeStruct((512, 128...]
    dot_general x54 -> x0, matrix products: 48 us -> none  [the longest x27 25.7 us: apply(): jnp.einsum(spec, values, matrix, precision=exact, preferred_element_type=...]
    dynamic_slice x24 -> x0, local copies, waits for them, and re-layouts: 19.4 us -> none  [the longest x8 7.36 us: spectrum_of(): inputs = lax.dynamic_slice_in_dim(signal, start, block, 1)]
    slice x40 -> x0, local copies, waits for them, and re-layouts: 18.1 us -> none  [the longest x32 18 us: mirror(): head = jnp.roll(shifted[..., 0, :, :], 1, axis=-2)]
    another operation x17 -> x0, local copies, waits for them, and re-layouts: 12.3 us -> none
    all_to_all x1 -> x0, waiting for transfers between devices: 10.5 us -> none  [joined_exchange(): lax.all_to_all(blocks, axis, split_axis=0, concat_axis=0, tiled=True)]
    all_to_all x1 -> x0, starting transfers between devices: 9.33 us -> none  [joined_exchange(): lax.all_to_all(blocks, axis, split_axis=0, concat_axis=0, tiled=True)]
  transfers between devices with their start and end apart: 2 -> 0, of which waited for: 2 -> 0; matrix products, arithmetic and copies ran while one was open for 1% -> 0% of each run, Pallas kernels for 0% -> 0%
where the time goes in v1:
time: 111 us
  Pallas kernels  48.3 us (44%)
  blocking collectives  40.8 us (37%)
  local copies, waits for them, and re-layouts  8.71 us (8%)
  other arithmetic  7.33 us (7%)
  matrix products  4.09 us (4%)
  between operations  1.23 us (1%)
    pallas_call x1, Pallas kernels, correlate(): pl.pallas_call(correlate_kernel, out_shape=jax.ShapeDtypeStruct((512, 128...  48.3 us
    all_to_all x2, blocking collectives, copy_for_each(): lax.all_to_all(jnp.broadcast_to(x[None], (peers, *x.shape)), axis, 0, 0,...  19.8 us
    all_to_all x1, blocking collectives, summed_rows(): lax.all_to_all(nearer, far, split_axis=0, concat_axis=0, tiled=True)  17.2 us
    sin x16, other arithmetic, lag_features(): sines.append(jnp.sin(phase))  6.93 us
    unnamed x72, local copies, waits for them, and re-layouts  4.41 us
    all_to_all x1, blocking collectives, sum_at_owner(): lax.all_to_all(blocks, axis, split_axis=0, concat_axis=0, tiled=True)  3.8 us
    slice x7, local copies, waits for them, and re-layouts, together(): finished.append(running[at:at + a.size].reshape(a.shape))  2.73 us

profile of v1, /device:TPU:1, one launch (start us, length us, event | category | flops | bytes accessed | tf_op | source)
XLA Modules:
  0.0 110.5 jit_solution(13100496968416632794)
XLA Ops:
  1.1 0.6 fusion.106
  1.6 0.6 fusion.104
  2.2 0.6 fusion.102
  3.3 0.6 fusion.98
  3.9 0.6 fusion.96
  4.6 0.6 fusion.94
  5.2 0.6 fusion.92
  5.8 0.6 fusion.90
  6.4 0.6 fusion.88
  7.0 0.6 fusion.86
  7.7 1.5 %copy.48 = bf16[8,8,64,128]{3,2,1,0:T(8,128)(2,1)S(1)} copy(bf16[8,8,64,128]{3,1,2,0:T(8,128)(2,1)} %bitcast.50) | data formatting | bytes 2097152
  11.2 48.3 %shard_map.180 = f32[512,128]{1,0:T(8,128)S(1)} custom-call(bf16[16,4,2,64,128]{4,3,2,1,0:T(8,128)(2,1)S(1)} %pad_maximum_fusion.both, bf16[128,128]{1,0:T(8,128)(2,1)S(1)} %copy-done.5, f32[2,64,128]{2,1,0:T(8,128)S(1)} %copy-done.4, bf16[768,256]{1,0:T(8,128)(2,1)S(1)} %copy-done.1, bf16[768,256]{1,0:T(8,128)(2,1)S(1)} %copy-done.2, ...), custom_call_target="tpu_custom_call" | custom-call | tf_op jit(solution)/shard_map/pallas_call | solution.py:222
  60.0 1.1 %multiply_reduce_fusion = (f32[64]{0:T(128)S(1)}, f32[64]{0:T(128)S(1)}, f32[64,128]{1,0:T(8,128)S(1)}) fusion(f32[64,128]{1,0:T(8,128)S(1)} %fusion.5, f32[64]{0:T(128)S(1)} %get-tuple-element.38, f32[64,64]{1,0:T(8,128)} %param.17, f32[64,128]{1,0:T(8,128)S(1)} %get-tuple-element.41, f32[64]{0:T(128)S(1)} %get-tuple-element.37), kind=kOutput, calls=%fused_computation.25 | convolution fusion | flops 6348672 | bytes 115712 | tf_op jit(solution)/shard_map/transpose(jvp())/dot_general | solution.py:332
  62.8 0.7 fusion.3
  63.9 3.8 %all_to_all.25 = f32[2,64,310]{2,1,0:T(8,128)S(1)} all-to-all(f32[2,64,310]{2,1,0:T(8,128)S(1)} %copy.38), channel_id=1, replica_groups=mesh['y'=4,'x'=4,'z'=4,'core'=2] {'core'}, dimensions={0} | all-to-all | bytes 317440 | tf_op jit(solution)/shard_map/all_to_all | solution.py:262
  67.8 17.2 %all_to_all.26 = f32[64,1,310]{2,1,0:T(1,128)S(1)} all-to-all(f32[64,1,310]{2,1,0:T(1,128)S(1)} %all_to_all.17), channel_id=1, replica_groups=mesh['y'=4,'x'=4,'z'=4,'core'=2] {'y','x','z'}, dimensions={0} | all-to-all | bytes 158720 | tf_op jit(solution)/shard_map/all_to_all | solution.py:270
  85.2 13.4 %all_to_all.28 = f32[64,1,310]{2,1,0:T(1,128)S(1)} all-to-all(f32[64,1,310]{2,1,0:T(1,128)S(1)} %broadcast_in_dim.33), channel_id=1, replica_groups=mesh['y'=4,'x'=4,'z'=4,'core'=2] {'y','x','z'}, dimensions={0} | all-to-all | bytes 158720 | tf_op jit(solution)/shard_map/all_to_all | solution.py:281
  98.6 6.4 %all_to_all.27 = f32[2,64,310]{2,1,0:T(8,128)S(1)} all-to-all(f32[2,64,310]{2,1,0:T(8,128)S(1)} %broadcast_in_dim.35), channel_id=1, replica_groups=mesh['y'=4,'x'=4,'z'=4,'core'=2] {'core'}, dimensions={0} | all-to-all | bytes 317440 | tf_op jit(solution)/shard_map/all_to_all | solution.py:281
  105.5 0.6 slice.39
  106.4 0.6 slice.40
  107.6 0.6 slice.43
  108.3 0.7 copy.41
  109.0 0.8 copy.42
  109.8 0.7 copy.52
  (108 shorter events, 6.8 us)
Async XLA Ops:
  0.6 58.9 %copy-start = (f32[512,64]{0,1:T(8,128)S(1)}, f32[512,64]{0,1:T(8,128)}, u32[]{:S(2)}) copy-start(f32[512,64]{0,1:T(8,128)} %param.19) | copy-start | bytes 393220
  0.6 8.6 %copy-start.6 = (bf16[1,64,8192]{2,1,0:T(8,128)(2,1)S(1)}, bf16[1,64,8192]{2,1,0:T(8,128)(2,1)}, u32[]{:S(2)}) copy-start(bf16[1,64,8192]{2,1,0:T(8,128)(2,1)} %param.13) | copy-start | bytes 3145732
  7.7 1.8 %copy-start.9 = (f32[2,64]{1,0:T(2,128)S(1)}, f32[2,64]{1,0:T(2,128)}, u32[]{:S(2)}) copy-start(f32[2,64]{1,0:T(2,128)} %param.18) | copy-start | bytes 1540
  7.7 1.8 %copy-start.8 = (f32[512]{0:T(512)S(1)}, f32[512]{0:T(512)}, u32[]{:S(2)}) copy-start(f32[512]{0:T(512)} %param.20) | copy-start | bytes 6148
  9.6 0.7 copy-start.12
  9.6 0.7 copy-start.13
  9.6 0.7 copy-start.14
  9.6 0.7 copy-start.15
  9.6 0.7 copy-start.16
  9.6 0.7 copy-start.17
  9.6 0.7 copy-start.18
  9.7 0.7 copy-start.19
  9.7 0.7 copy-start.20
  9.7 0.7 copy-start.21
  9.7 0.7 copy-start.28
  9.8 0.7 copy-start.30
  9.8 0.8 copy-start.31
  9.8 0.8 copy-start.32
  9.8 1.0 copy-start.7
  9.8 1.3 %copy-start.1 = (bf16[768,256]{1,0:T(8,128)(2,1)S(1)}, bf16[768,256]{1,0:T(8,128)(2,1)}, u32[]{:S(2)}) copy-start(bf16[768,256]{1,0:T(8,128)(2,1)} %constant.171.clone.forward) | copy-start | bytes 1179652
  9.8 1.3 %copy-start.2 = (bf16[768,256]{1,0:T(8,128)(2,1)S(1)}, bf16[768,256]{1,0:T(8,128)(2,1)}, u32[]{:S(2)}) copy-start(bf16[768,256]{1,0:T(8,128)(2,1)} %constant.172.clone.backward) | copy-start | bytes 1179652
  9.8 1.3 %copy-start.3 = (bf16[128,384]{1,0:T(8,128)(2,1)S(1)}, bf16[128,384]{1,0:T(8,128)(2,1)}, u32[]{:S(2)}) copy-start(bf16[128,384]{1,0:T(8,128)(2,1)} %constant.173.clone.last) | copy-start | bytes 294916
  9.8 1.3 %copy-start.4 = (f32[2,64,128]{2,1,0:T(8,128)S(1)}, f32[2,64,128]{2,1,0:T(8,128)}, u32[]{:S(2)}) copy-start(f32[2,64,128]{2,1,0:T(8,128)} %constant.170.clone.twist) | copy-start | bytes 196612
  9.9 1.3 %copy-start.5 = (bf16[128,128]{1,0:T(8,128)(2,1)S(1)}, bf16[128,128]{1,0:T(8,128)(2,1)}, u32[]{:S(2)}) copy-start(bf16[128,128]{1,0:T(8,128)(2,1)} %constant.169.clone.first) | copy-start | bytes 98308
  (9 other events, 5.9 us)

commit v2 on v1

v2 whole, which is shorter than its diff:
```python
import math

import jax
import jax.numpy as jnp
import numpy as np
from jax import lax
from jax.experimental import pallas as pl
from jax.experimental.pallas import tpu as pltpu
from jax.sharding import Mesh
from jax.sharding import PartitionSpec as P

DP = ("y", "x")
CHAN = ("z", "core")
MESH_ID = pl.DeviceIdType.MESH
OFFSETS = sorted(
    [(dy, dx) for dy in range(4) for dx in range(4)],
    key=lambda p: (min(p[0], 4 - p[0]) + min(p[1], 4 - p[1])),
)
PEERS = [(dz, dc) for dz in range(4) for dc in range(2)]


def split_table(values):
    high = values.astype(jnp.bfloat16)
    low = (values - high.astype(np.float64)).astype(jnp.bfloat16)
    return high, low


def transform_tables(total, scale):
    half, side = 64, 128
    k1 = np.arange(half)[:, None] + 0.5
    n1 = np.arange(half)[None, :]
    angle = -2.0 * np.pi * k1 * n1 / side
    first = np.concatenate([np.cos(angle), np.sin(angle)], axis=0)
    first = np.concatenate(split_table(first), axis=1)
    n2 = np.arange(side)[None, :]
    angle = -2.0 * np.pi * k1 * n2 / total
    twist = np.stack([np.cos(angle), np.sin(angle)]).astype(np.float32)
    rows = np.arange(side)[:, None]
    angle = -2.0 * np.pi * (rows * n2 % side) / side
    cosine, sine = np.cos(angle), np.sin(angle)
    forward = np.block([[cosine, sine], [-sine, cosine]])
    high, low = split_table(forward)
    forward = np.concatenate([high, high, low], axis=0)
    backward = np.block([[cosine, -sine], [sine, cosine]])
    high, low = split_table(backward)
    backward = np.concatenate([high, high, low], axis=0)
    lag_row = np.arange(side)[:, None]
    freq = np.arange(half)[None, :] + 0.5
    angle = 2.0 * np.pi * lag_row * freq / side
    last = np.concatenate([np.cos(angle), -np.sin(angle)], axis=1)
    last = last * np.where(lag_row < half, 1.0, -1.0) * (2.0 * scale / total)
    high, low = split_table(last)
    last = np.concatenate([high, high, low], axis=1)
    return first, twist, forward, backward, last


def split_values(values):
    high = values.astype(jnp.bfloat16)
    low = (values - high.astype(jnp.float32)).astype(jnp.bfloat16)
    return high, low


def dot(a, b):
    return jnp.dot(a, b, preferred_element_type=jnp.float32)


def exact_dot(a, b, dims=((1,), (0,))):
    return lax.dot_general(
        a, b, (dims, ((), ())), precision=lax.Precision.HIGHEST, preferred_element_type=jnp.float32
    )


def sine_cosine(angle):
    turns = jnp.floor(angle * (2.0 / math.pi) + 0.5)
    rest = angle - turns * 1.5703125
    rest = rest - turns * 4.837512969970703125e-4
    rest = rest - turns * 7.54978995489188216e-8
    square = rest * rest
    sine = -1.9515295891e-4 * square + 8.3321608736e-3
    sine = sine * square - 1.6666654611e-1
    sine = sine * square * rest + rest
    cosine = 2.443315711809948e-5 * square - 1.388731625493765e-3
    cosine = cosine * square + 4.166664568298827e-2
    cosine = cosine * square * square - 0.5 * square + 1.0
    quarter = turns.astype(jnp.int32)
    odd = (quarter & 1) == 1
    first = jnp.where(odd, cosine, sine)
    second = jnp.where(odd, sine, cosine)
    first = jnp.where((quarter & 2) == 2, -first, first)
    second = jnp.where(((quarter + 1) & 2) == 2, -second, second)
    return first, second


def as_columns(row):
    return jnp.broadcast_to(row, (128, row.shape[1])).T


def kernel(
    both,
    first,
    twist,
    forward,
    backward,
    last,
    bands,
    embed_weight,
    embed_bias,
    hidden_weight,
    frequency,
    output_weight,
    decay_rate,
    filter_out,
    embed_out,
    bias_out,
    hidden_out,
    frequency_out,
    output_out,
    decay_out,
    arrived,
    spectrum,
    lags,
    mine,
    rows,
    landed,
    table,
    embed_pad,
    decay_columns,
    pre_first,
    sine_first,
    cosine_first,
    pre_second,
    sine_second,
    cosine_second,
    window,
    slope,
    partial,
    partials,
    own_sum,
    group_sums,
    piece,
    pieces,
    local_sem,
    dp_send,
    dp_recv,
    chan_send,
    chan_recv,
):
    y, x = lax.axis_index("y"), lax.axis_index("x")
    z, core = lax.axis_index("z"), lax.axis_index("core")
    me = y * 4 + x
    group = z * 2 + core

    barrier = pltpu.get_barrier_semaphore()
    dp_peers = []
    for dy, dx in OFFSETS[1:]:
        ty, tx = lax.rem(y + dy, 4), lax.rem(x + dx, 4)
        dp_peers.append((ty * 4 + tx, {"y": ty, "x": tx}))
    chan_peers = []
    for dz, dc in PEERS[1:]:
        tz, tc = lax.rem(z + dz, 4), lax.rem(core + dc, 2)
        chan_peers.append((tz * 2 + tc, {"z": tz, "core": tc}))
    for _, where in dp_peers + chan_peers:
        pl.semaphore_signal(barrier, 1, device_id=where, device_id_type=MESH_ID)
    own = pltpu.make_async_copy(both.at[me], arrived.at[0], local_sem)
    own.start()
    spectrum[...] = jnp.zeros_like(spectrum)
    pl.semaphore_wait(barrier, len(dp_peers) + len(chan_peers))

    def exchange(stage, peers, sends, recvs, source, target):
        copies = []
        for at, (index, where) in enumerate(peers):
            copy = pltpu.make_async_remote_copy(
                source(index),
                target(at),
                sends.at[stage, at],
                recvs.at[stage, at],
                device_id=where,
                device_id_type=MESH_ID,
            )
            copy.start()
            copies.append(copy)
        return copies

    over_dp = lambda stage, source, target: exchange(
        stage, dp_peers, dp_send, dp_recv, source, target
    )
    over_chan = lambda stage, source, target: exchange(
        stage, chan_peers, chan_send, chan_recv, source, target
    )

    inputs = over_dp(0, lambda index: both.at[index], lambda at: arrived.at[at + 1])

    table[...] = jnp.zeros_like(table)
    embed_pad[...] = jnp.zeros_like(embed_pad)
    embed_pad[:, :33] = embed_weight[...]
    position = me * 1024 + lax.broadcasted_iota(jnp.int32, (16, 1024), 1)
    lag = jnp.where(me < 8, position, position - 16384)
    phase = ((lag * jnp.concatenate([bands[...]] * 8, axis=1)) & 16383).astype(jnp.float32)
    sines, cosines = sine_cosine(phase * (2.0 * math.pi / 16384))
    table[0:1, :] = lag[:1].astype(jnp.float32) * (1.0 / 8192)
    table[1:17, :] = sines
    table[17:33, :] = cosines
    wide = lambda columns: jnp.concatenate([columns] * 8, axis=1)
    bias = as_columns(jnp.concatenate([embed_bias[...]] * 2, axis=1))[:64]
    freq_rows = jnp.concatenate([frequency[...]] * 2, axis=1)
    freq_first, freq_second = as_columns(freq_rows[0:1])[:64], as_columns(freq_rows[1:2])[:64]
    before = exact_dot(embed_pad[...], table[...]) + wide(bias)
    pre_first[...] = before
    sine, cosine = sine_cosine(wide(freq_first) * before)
    sine_first[...] = sine
    cosine_first[...] = cosine
    before = exact_dot(hidden_weight[...], sine)
    pre_second[...] = before
    sine, cosine = sine_cosine(wide(freq_second) * before)
    sine_second[...] = sine
    cosine_second[...] = cosine
    decay_columns[...] = as_columns(decay_rate[...])
    weights = output_weight[pl.ds(pl.multiple_of(group * 64, 64), 64), :]
    decay = decay_columns[pl.ds(pl.multiple_of(group * 64, 64), 64), :]
    distance = jnp.abs(lag[:1]).astype(jnp.float32) * (1.0 / 8192)
    shape = jnp.exp(-wide(decay) * distance) * (1.0 / 128)
    window[...] = shape
    slope[...] = exact_dot(weights, sine) * shape * -distance

    cos_t, sin_t = twist[0], twist[1]

    def add_sequence(slot):
        parts = []
        for part in range(2):
            for channel in range(4):
                data = arrived[slot, channel, part]
                data = jnp.concatenate([data, data], axis=0)
                step = dot(first[...], data)
                real, imag = step[:64], step[64:]
                parts.append(
                    jnp.concatenate(
                        [real * cos_t - imag * sin_t, real * sin_t + imag * cos_t], axis=1
                    )
                )
        high, low = split_values(jnp.concatenate(parts, axis=0))
        whole = dot(jnp.concatenate([high, low, high], axis=1), forward[...])
        in_real, in_imag = whole[:256, :128], whole[:256, 128:]
        grad_real, grad_imag = whole[256:, :128], whole[256:, 128:]
        spectrum[:, :128] += in_real * grad_real + in_imag * grad_imag
        spectrum[:, 128:] += in_real * grad_imag - in_imag * grad_real

    own.wait()
    add_sequence(0)

    @pl.loop(0, 15)
    def _(at):
        pltpu.make_async_remote_copy(
            both.at[0],
            arrived.at[at + 1],
            dp_send.at[0, at],
            dp_recv.at[0, at],
            device_id={"y": y, "x": lax.rem(x + 1, 4)},
            device_id_type=MESH_ID,
        ).wait_recv()
        add_sequence(at + 1)

    high, low = split_values(spectrum[...])
    back = dot(jnp.concatenate([high, low, high], axis=1), backward[...])
    columns = []
    for channel in range(4):
        real = back[64 * channel : 64 * channel + 64, :128]
        imag = back[64 * channel : 64 * channel + 64, 128:]
        columns.append(
            jnp.concatenate([real * cos_t + imag * sin_t, imag * cos_t - real * sin_t], axis=0)
        )
    high, low = split_values(jnp.concatenate(columns, axis=1))
    result = dot(last[...], jnp.concatenate([high, low, high], axis=0))
    lags[...] = result.reshape(16, 8, 512)

    to_owner = over_dp(1, lambda index: lags.at[index], lambda at: mine.at[me])
    mine[me] = lags[me]
    for copy in to_owner:
        copy.wait_recv()
    for lag_row in range(8):
        for channel in range(4):
            rows[lag_row, pl.ds(channel, 16, stride=4), :] = mine[
                :, lag_row, 128 * channel : 128 * channel + 128
            ]
    to_row = over_chan(0, lambda index: rows.at[index], lambda at: landed.at[group])
    landed[group] = rows[group]

    lanes = ((1,), (1,))
    down = ((0,), (0,))
    ones = jnp.ones((8, 1024), jnp.float32)
    grad = jnp.concatenate([rows[lag_row] for lag_row in range(8)], axis=1)
    decay_row = exact_dot(ones, grad * slope[...], lanes)
    shaped = grad * window[...]
    output_grad = exact_dot(shaped, sine_second[...], lanes)
    turned = exact_dot(weights, shaped, down) * cosine_second[...]
    frequency_second = exact_dot(ones, turned * pre_second[...], lanes)
    turned = turned * wide(freq_second)
    hidden_grad = exact_dot(turned, sine_first[...], lanes)
    turned = exact_dot(hidden_weight[...], turned, down) * cosine_first[...]
    frequency_first = exact_dot(ones, turned * pre_first[...], lanes)
    turned = turned * wide(freq_first)
    bias_row = exact_dot(ones, turned, lanes)
    embed_grad = exact_dot(turned, table[...], lanes)

    shared = jnp.concatenate([hidden_grad, embed_grad[:, :64]], axis=1)
    for k in range(4):
        partial[:, k, :] = shared[16 * k : 16 * k + 16]
    packed = jnp.concatenate([output_grad[:32], output_grad[32:]], axis=1)
    for k in range(2):
        partial[:, 4 + k, :] = packed[16 * k : 16 * k + 16]
    vectors = jnp.concatenate([bias_row[:1], frequency_first[:1]], axis=1)
    partial[:, 6, :] = jnp.broadcast_to(vectors, (16, 128))
    vectors = jnp.concatenate([frequency_second[:1], decay_row[:1]], axis=1)
    partial[:, 7, :] = jnp.broadcast_to(vectors, (16, 128))
    to_sum = over_dp(2, lambda index: partial.at[index], lambda at: partials.at[me])
    partials[me] = partial[me]
    for copy in to_sum:
        copy.wait_recv()
    own_sum[...] = jnp.sum(partials[...], axis=0)
    to_groups = over_chan(1, lambda index: own_sum, lambda at: group_sums.at[group])
    group_sums[group] = own_sum[...]
    for copy in to_groups:
        copy.wait_recv()
    summed = jnp.sum(group_sums[...], axis=0)
    piece[0:4, :] = summed[0:4]
    piece[20:24, :] = jnp.zeros((4, 128), jnp.float32)
    for g in range(8):
        piece[4 + 2 * g : 6 + 2 * g, :] = group_sums[g, 4:6, :]
    to_all = over_dp(3, lambda index: piece, lambda at: pieces.at[me])
    pieces[me] = piece[...]
    bias_out[...] = summed[6:7, :64]
    frequency_out[0:1, :] = summed[6:7, 64:]
    frequency_out[1:2, :] = summed[7:8, :64]
    for g in range(8):
        decay_out[0:1, 64 * g : 64 * g + 64] = group_sums[g, 7:8, 64:]
    for copy in to_row:
        copy.wait_recv()
    filter_out[...] = landed[...].reshape(512, 128)
    for copy in to_all:
        copy.wait_recv()
    for k in range(4):
        block = pieces[:, k, :]
        hidden_out[16 * k : 16 * k + 16, :] = block[:, :64]
        embed_out[16 * k : 16 * k + 16, :] = block[:, 64:97]
    for g in range(8):
        for k in range(2):
            block = pieces[:, 4 + 2 * g + k, :]
            at = 64 * g + 16 * k
            output_out[at : at + 16, :] = block[:, :64]
            output_out[at + 32 : at + 48, :] = block[:, 64:]
    for copy in inputs + to_owner + to_row + to_sum + to_groups + to_all:
        copy.wait_send()


def local(
    signal,
    signal_grad,
    embed_weight,
    embed_bias,
    hidden_weight,
    frequency,
    output_weight,
    decay_rate,
):
    total = 2 * signal.shape[2]
    scale = 1.0 / math.sqrt(16 * signal.shape[2])
    both = jnp.stack(
        [signal.reshape(16, 4, 64, 128), signal_grad.reshape(16, 4, 64, 128)], axis=2
    )
    factors = [max(1, int(0.45 * total * 10000.0 ** (-band / 16))) for band in range(16)]
    bands = np.repeat(np.array(factors, np.int32)[:, None], 128, axis=1)
    tables = transform_tables(total, scale)
    vmem = pl.BlockSpec(memory_space=pltpu.VMEM)
    f32 = jnp.float32
    lags = pltpu.VMEM((64, 1024), f32)
    outs = pl.pallas_call(
        kernel,
        out_shape=[
            jax.ShapeDtypeStruct(shape, f32)
            for shape in [(512, 128), (64, 33), (1, 64), (64, 64), (2, 64), (512, 64), (1, 512)]
        ],
        in_specs=[pl.BlockSpec(memory_space=pl.ANY)] + [vmem] * 12,
        out_specs=[vmem] * 7,
        scratch_shapes=[
            pltpu.VMEM((16, 4, 2, 64, 128), jnp.bfloat16),
            pltpu.VMEM((256, 256), f32),
            pltpu.VMEM((16, 8, 512), f32),
            pltpu.VMEM((16, 8, 512), f32),
            pltpu.VMEM((8, 64, 128), f32),
            pltpu.VMEM((8, 64, 128), f32),
            pltpu.VMEM((128, 1024), f32),
            pltpu.VMEM((64, 128), f32),
            pltpu.VMEM((512, 128), f32),
            *[lags] * 8,
            pltpu.VMEM((16, 8, 128), f32),
            pltpu.VMEM((16, 8, 128), f32),
            pltpu.VMEM((8, 128), f32),
            pltpu.VMEM((8, 8, 128), f32),
            pltpu.VMEM((24, 128), f32),
            pltpu.VMEM((16, 24, 128), f32),
            pltpu.SemaphoreType.DMA,
            pltpu.SemaphoreType.DMA((4, 15)),
            pltpu.SemaphoreType.DMA((4, 15)),
            pltpu.SemaphoreType.DMA((2, 7)),
            pltpu.SemaphoreType.DMA((2, 7)),
        ],
        compiler_params=pltpu.CompilerParams(
            collective_id=0, has_side_effects=True, vmem_limit_bytes=40 * 1024 * 1024
        ),
    )(
        both,
        *[jnp.asarray(t) for t in tables],
        jnp.asarray(bands),
        embed_weight,
        embed_bias.reshape(1, 64),
        hidden_weight,
        frequency,
        output_weight,
        decay_rate.reshape(1, 512),
    )
    lag_grad, embed_grad, bias_grad, hidden_grad, frequency_grad, output_grad, decay_grad = outs
    return (
        lag_grad,
        embed_grad,
        bias_grad.reshape(64),
        hidden_grad,
        frequency_grad,
        output_grad,
        decay_grad.reshape(512),
    )


def solution(mesh):
    torus = Mesh(mesh.devices.reshape(4, 4, 4, 2), ("y", "x", "z", "core"))
    return jax.shard_map(
        local,
        mesh=torus,
        in_specs=(P(DP, CHAN, None), P(DP, CHAN, None), P(), P(), P(), P(), P(), P()),
        out_specs=(P(None, DP + CHAN), P(), P(), P(), P(), P(), P()),
        check_vma=False,
    )
```

time: 111 us -> 80.7 us (0.73)
  blocking collectives: 40.8 us -> 0 us
  Pallas kernels: 48.3 us -> 61.4 us
  local copies, waits for them, and re-layouts: 8.71 us -> 17.7 us
  other arithmetic: 7.33 us -> 0.19 us
  matrix products: 4.09 us -> 0 us
    all_to_all x4 -> x0, blocking collectives: 40.8 us -> none  [the longest x2 19.8 us: copy_for_each(): lax.all_to_all(jnp.broadcast_to(x[None], (peers, *x.shape)), axis, 0, 0,...]
    unnamed x72 -> x47, local copies, waits for them, and re-layouts: 4.41 us -> 17.7 us
    pallas_call x1, Pallas kernels: 48.3 us -> 61.4 us  [local(): pl.pallas_call(kernel, out_shape=[jax.ShapeDtypeStruct(shape, f32) for sh...]
    sin x16 -> x0, other arithmetic: 6.93 us -> none  [lag_features(): sines.append(jnp.sin(phase))]
    dot_general x8 -> x0, matrix products: 4.09 us -> none  [the longest x3 1.86 us: filter_loss(): jnp.dot(hidden_weight, first, precision=exact, preferred_element_type=jnp...]
    slice x7 -> x0, local copies, waits for them, and re-layouts: 2.73 us -> none  [together(): finished.append(running[at:at + a.size].reshape(a.shape))]
where the time goes in v2:
time: 80.7 us; the launch traced here: 80.1 us
  Pallas kernels  61.4 us (76%)
  local copies, waits for them, and re-layouts  17.7 us (22%)
    pallas_call x1, Pallas kernels, local(): pl.pallas_call(kernel, out_shape=[jax.ShapeDtypeStruct(shape, f32) for sh...  61.4 us
    unnamed x47, local copies, waits for them, and re-layouts  17.7 us

profile of v2, /device:TPU:1, one launch (start us, length us, event | category | flops | bytes accessed | tf_op | source)
XLA Modules:
  0.0 80.1 jit_solution(17078053239446093961)
XLA Ops:
  0.6 1.6 %copy.26 = bf16[8,8,64,128]{3,2,1,0:T(8,128)(2,1)S(1)} copy(bf16[8,8,64,128]{3,1,2,0:T(8,128)(2,1)} %bitcast.18) | data formatting | bytes 2097152
  2.2 0.3 copy.25
  2.6 0.2 pad_maximum_fusion.both
  2.8 0.6 copy-done.16
  3.4 0.1 copy.22.output_weight
  3.6 0.1 copy.21.embed_weight
  3.8 0.8 %copy-done.4 = f32[2,64,128]{2,1,0:T(8,128)S(1)} copy-done((f32[2,64,128]{2,1,0:T(8,128)S(1)}, f32[2,64,128]{2,1,0:T(8,128)}, u32[]{:S(2)}) %copy-start.4) | copy-done | bytes 65560
  4.6 0.8 copy-done.5
  5.4 0.8 copy-done.6
  6.1 0.7 copy-done.11
  6.8 0.7 copy-done.13
  7.4 61.4 %shard_map.189 = (f32[512,128]{1,0:T(8,128)S(1)}, f32[64,33]{1,0:T(8,128)S(1)}, f32[1,64]{1,0:T(1,128)S(1)}, f32[64,64]{1,0:T(8,128)S(1)}, f32[2,64]{1,0:T(2,128...) custom-call(bf16[16,4,2,64,128]{4,3,2,1,0:T(8,128)(2,1)S(1)} %pad_maximum_fusion.both, ...), custom_call_target="tpu_custom_call" | custom-call | tf_op jit(solution)/shard_map/pallas_call | solution.py:375
  68.9 0.7 copy-done.2
  69.6 0.6 copy-done.7
  70.2 0.6 copy-done.8
  70.8 0.6 copy-done.12
  71.4 0.5 copy-done.14
  71.9 0.8 copy.24
  72.6 1.4 %copy.23 = f32[64,33]{0,1:T(8,128)} copy(f32[64,33]{1,0:T(8,128)} %copy-done.8) | data formatting | bytes 16896
  74.1 1.7 %copy.32 = f32[512,128]{1,0:T(8,128)} copy(f32[512,128]{1,0:T(8,128)} %copy-done.2) | data formatting | bytes 524288
  75.7 1.2 %copy.33 = f32[64]{0:T(128)} copy(f32[64]{0:T(128)} %bitcast.15) | data formatting | bytes 512
  76.9 1.4 %copy.34 = f32[64,64]{1,0:T(8,128)} copy(f32[64,64]{1,0:T(8,128)} %copy-done.7) | data formatting | bytes 32768
  78.3 1.2 %copy.35 = f32[2,64]{1,0:T(2,128)} copy(f32[2,64]{1,0:T(2,128)} %copy-done.12) | data formatting | bytes 1024
  79.5 0.6 copy.36
  (25 shorter events, 0.1 us)
Async XLA Ops:
  0.6 1.6 %copy-start.15 = (bf16[1,64,8192]{2,1,0:T(8,128)(2,1)S(1)}, bf16[1,64,8192]{2,1,0:T(8,128)(2,1)}, u32[]{:S(2)}) copy-start(bf16[1,64,8192]{2,1,0:T(8,128)(2,1)} %param.14) | copy-start | bytes 3145732
  2.5 0.9 %copy-start.16 = (f32[512,64]{0,1:T(8,128)S(1)}, f32[512,64]{0,1:T(8,128)}, u32[]{:S(2)}) copy-start(f32[512,64]{0,1:T(8,128)} %param.20) | copy-start | bytes 393220
  2.5 1.0 %copy-start.17 = (f32[64,33]{0,1:T(8,128)S(1)}, f32[64,33]{0,1:T(8,128)}, u32[]{:S(2)}) copy-start(f32[64,33]{0,1:T(8,128)} %param.16) | copy-start | bytes 25348
  2.5 1.1 %copy-start = (bf16[768,256]{1,0:T(8,128)(2,1)S(1)}, bf16[768,256]{1,0:T(8,128)(2,1)}, u32[]{:S(2)}) copy-start(bf16[768,256]{1,0:T(8,128)(2,1)} %constant.14.clone.forward) | copy-start | bytes 1179652
  2.6 1.2 %copy-start.1 = (bf16[768,256]{1,0:T(8,128)(2,1)S(1)}, bf16[768,256]{1,0:T(8,128)(2,1)}, u32[]{:S(2)}) copy-start(bf16[768,256]{1,0:T(8,128)(2,1)} %constant.15.clone.backward) | copy-start | bytes 1179652
  2.6 1.2 %copy-start.3 = (bf16[128,384]{1,0:T(8,128)(2,1)S(1)}, bf16[128,384]{1,0:T(8,128)(2,1)}, u32[]{:S(2)}) copy-start(bf16[128,384]{1,0:T(8,128)(2,1)} %constant.16.clone.last) | copy-start | bytes 294916
  2.6 1.2 %copy-start.9 = (s32[16,128]{1,0:T(8,128)S(1)}, s32[16,128]{1,0:T(8,128)}, u32[]{:S(2)}) copy-start(s32[16,128]{1,0:T(8,128)} %constant.17.clone.bands) | copy-start | bytes 24580
  2.6 1.2 %copy-start.10 = (f32[512]{0:T(512)S(1)}, f32[512]{0:T(512)}, u32[]{:S(2)}) copy-start(f32[512]{0:T(512)} %param.21) | copy-start | bytes 6148
  3.8 0.8 %copy-start.4 = (f32[2,64,128]{2,1,0:T(8,128)S(1)}, f32[2,64,128]{2,1,0:T(8,128)}, u32[]{:S(2)}) copy-start(f32[2,64,128]{2,1,0:T(8,128)} %constant.13.clone.twist) | copy-start | bytes 196612
  4.6 0.8 copy-start.5
  5.4 0.8 copy-start.6
  6.1 0.7 copy-start.11
  6.8 0.7 copy-start.13
  68.8 0.7 copy-start.2
  69.6 0.6 copy-start.7
  70.2 0.6 copy-start.8
  70.8 0.6 copy-start.12
  71.3 0.5 copy-start.14

commit v3 on v2

--- a/solution.py
+++ b/solution.py
@@ -16,7 +16,9 @@
     [(dy, dx) for dy in range(4) for dx in range(4)],
     key=lambda p: (min(p[0], 4 - p[0]) + min(p[1], 4 - p[1])),
 )
-PEERS = [(dz, dc) for dz in range(4) for dc in range(2)]
+PEERS = sorted(
+    [(dz, dc) for dz in range(4) for dc in range(2)], key=lambda p: (min(p[0], 4 - p[0]) + p[1])
+)
 
 
 def split_table(values):
@@ -96,55 +98,59 @@
 
 
 def kernel(
-    both,
-    first,
-    twist,
-    forward,
-    backward,
-    last,
-    bands,
-    embed_weight,
-    embed_bias,
-    hidden_weight,
-    frequency,
-    output_weight,
-    decay_rate,
-    filter_out,
-    embed_out,
-    bias_out,
-    hidden_out,
-    frequency_out,
-    output_out,
-    decay_out,
-    arrived,
-    spectrum,
-    lags,
-    mine,
-    rows,
-    landed,
-    table,
-    embed_pad,
-    decay_columns,
-    pre_first,
-    sine_first,
-    cosine_first,
-    pre_second,
-    sine_second,
-    cosine_second,
-    window,
-    slope,
-    partial,
-    partials,
-    own_sum,
-    group_sums,
-    piece,
-    pieces,
-    local_sem,
-    dp_send,
-    dp_recv,
-    chan_send,
-    chan_recv,
+    signal,
+    signal_grad,
+    *refs,
 ):
+    (
+        *stored,
+        landed,
+        pieces,
+        group_sums,
+        first,
+        twist,
+        forward,
+        backward,
+        last,
+        bands,
+        embed_weight,
+        embed_bias,
+        hidden_weight,
+        frequency,
+        output_weight,
+        decay_rate,
+        natural,
+        spread,
+        both,
+        arrived,
+        spectrum,
+        lags,
+        mine,
+        rows,
+        table,
+        embed_pad,
+        decay_columns,
+        output_rows,
+        pre_first,
+        sine_first,
+        cosine_first,
+        pre_second,
+        sine_second,
+        cosine_second,
+        window,
+        slope,
+        partial,
+        partials,
+        own_sum,
+        piece,
+        local_sem,
+        input_sem,
+        table_sem,
+        dp_send,
+        dp_recv,
+        chan_send,
+        chan_recv,
+    ) = refs
     y, x = lax.axis_index("y"), lax.axis_index("x")
     z, core = lax.axis_index("z"), lax.axis_index("core")
     me = y * 4 + x
@@ -159,16 +165,43 @@
     for dz, dc in PEERS[1:]:
         tz, tc = lax.rem(z + dz, 4), lax.rem(core + dc, 2)
         chan_peers.append((tz * 2 + tc, {"z": tz, "core": tc}))
-    for _, where in dp_peers + chan_peers:
+    for _, where in dp_peers[::-1] + chan_peers[::-1]:
         pl.semaphore_signal(barrier, 1, device_id=where, device_id_type=MESH_ID)
+    loads = []
+    for part, source in enumerate((signal, signal_grad)):
+        loads.append(pltpu.make_async_copy(source, natural.at[part], input_sem.at[part]))
+        loads[-1].start()
+    fetches = []
+    for at, source in enumerate(stored):
+        fetches.append(pltpu.make_async_copy(source, refs[15 + at], table_sem.at[at]))
+        fetches[-1].start()
+    spectrum[...] = jnp.zeros_like(spectrum)
+
+    for part in range(2):
+        loads[part].wait()
+
+        @pl.loop(0, 4)
+        def _(block):
+            for tile in range(64):
+                piece_of = natural[
+                    part, pl.ds(pl.multiple_of(block * 16, 16), 16), 128 * tile : 128 * tile + 128
+                ]
+                spread[pl.ds(tile, 16, stride=72), :] = piece_of.astype(jnp.float32)
+            for peer in range(4):
+                for channel in range(4):
+                    at = 72 * (4 * peer + channel)
+                    both[4 * block + peer, channel, part] = spread[at : at + 64, :].astype(
+                        jnp.bfloat16
+                    )
+
     own = pltpu.make_async_copy(both.at[me], arrived.at[0], local_sem)
     own.start()
-    spectrum[...] = jnp.zeros_like(spectrum)
     pl.semaphore_wait(barrier, len(dp_peers) + len(chan_peers))
 
-    def exchange(stage, peers, sends, recvs, source, target):
+    def exchange(stage, peers, sends, recvs, source, target, whole=False):
         copies = []
-        for at, (index, where) in enumerate(peers):
+        order = list(enumerate(peers))
+        for at, (index, where) in order if whole else order[::-1]:
             copy = pltpu.make_async_remote_copy(
                 source(index),
                 target(at),
@@ -182,7 +215,7 @@
         return copies
 
     over_dp = lambda stage, source, target: exchange(
-        stage, dp_peers, dp_send, dp_recv, source, target
+        stage, dp_peers, dp_send, dp_recv, source, target, stage == 0
     )
     over_chan = lambda stage, source, target: exchange(
         stage, chan_peers, chan_send, chan_recv, source, target
@@ -190,9 +223,12 @@
 
     inputs = over_dp(0, lambda index: both.at[index], lambda at: arrived.at[at + 1])
 
+    for fetch in fetches:
+        fetch.wait()
+
     table[...] = jnp.zeros_like(table)
     embed_pad[...] = jnp.zeros_like(embed_pad)
-    embed_pad[:, :33] = embed_weight[...]
+    embed_pad[:33, :] = embed_weight[...]
     position = me * 1024 + lax.broadcasted_iota(jnp.int32, (16, 1024), 1)
     lag = jnp.where(me < 8, position, position - 16384)
     phase = ((lag * jnp.concatenate([bands[...]] * 8, axis=1)) & 16383).astype(jnp.float32)
@@ -204,7 +240,7 @@
     bias = as_columns(jnp.concatenate([embed_bias[...]] * 2, axis=1))[:64]
     freq_rows = jnp.concatenate([frequency[...]] * 2, axis=1)
     freq_first, freq_second = as_columns(freq_rows[0:1])[:64], as_columns(freq_rows[1:2])[:64]
-    before = exact_dot(embed_pad[...], table[...]) + wide(bias)
+    before = exact_dot(embed_pad[...], table[...], ((0,), (0,))) + wide(bias)
     pre_first[...] = before
     sine, cosine = sine_cosine(wide(freq_first) * before)
     sine_first[...] = sine
@@ -215,7 +251,8 @@
     sine_second[...] = sine
     cosine_second[...] = cosine
     decay_columns[...] = as_columns(decay_rate[...])
-    weights = output_weight[pl.ds(pl.multiple_of(group * 64, 64), 64), :]
+    output_rows[...] = output_weight[...].T
+    weights = output_rows[pl.ds(pl.multiple_of(group * 64, 64), 64), :]
     decay = decay_columns[pl.ds(pl.multiple_of(group * 64, 64), 64), :]
     distance = jnp.abs(lag[:1]).astype(jnp.float32) * (1.0 / 8192)
     shape = jnp.exp(-wide(decay) * distance) * (1.0 / 128)
@@ -327,28 +364,66 @@
         piece[4 + 2 * g : 6 + 2 * g, :] = group_sums[g, 4:6, :]
     to_all = over_dp(3, lambda index: piece, lambda at: pieces.at[me])
     pieces[me] = piece[...]
-    bias_out[...] = summed[6:7, :64]
-    frequency_out[0:1, :] = summed[6:7, 64:]
-    frequency_out[1:2, :] = summed[7:8, :64]
-    for g in range(8):
-        decay_out[0:1, 64 * g : 64 * g + 64] = group_sums[g, 7:8, 64:]
-    for copy in to_row:
+    for copy in to_row + to_all:
         copy.wait_recv()
-    filter_out[...] = landed[...].reshape(512, 128)
-    for copy in to_all:
-        copy.wait_recv()
-    for k in range(4):
-        block = pieces[:, k, :]
-        hidden_out[16 * k : 16 * k + 16, :] = block[:, :64]
-        embed_out[16 * k : 16 * k + 16, :] = block[:, 64:97]
+    for copy in inputs + to_owner + to_row + to_sum + to_groups + to_all:
+        copy.wait_send()
+
+
+def finish(
+    landed,
+    pieces,
+    group_sums,
+    filter_out,
+    embed_out,
+    bias_out,
+    hidden_out,
+    frequency_out,
+    output_out,
+    decay_out,
+    embed,
+    bias,
+    hidden,
+    frequency,
+    output_rows,
+    output,
+    decay,
+    sems,
+):
+    copies = [pltpu.make_async_copy(landed, filter_out, sems.at[0])]
+    copies[0].start()
+
+    def send(source, target):
+        copies.append(pltpu.make_async_copy(source, target, sems.at[len(copies)]))
+        copies[-1].start()
+
     for g in range(8):
         for k in range(2):
             block = pieces[:, 4 + 2 * g + k, :]
             at = 64 * g + 16 * k
-            output_out[at : at + 16, :] = block[:, :64]
-            output_out[at + 32 : at + 48, :] = block[:, 64:]
-    for copy in inputs + to_owner + to_row + to_sum + to_groups + to_all:
-        copy.wait_send()
+            output_rows[at : at + 16, :] = block[:, :64]
+            output_rows[at + 32 : at + 48, :] = block[:, 64:]
+    output[...] = output_rows[...].T
+    send(output, output_out)
+    rows = []
+    for k in range(4):
+        block = pieces[:, k, :]
+        hidden[16 * k : 16 * k + 16, :] = block[:, :64]
+        rows.append(block)
+    send(hidden, hidden_out)
+    embed[...] = jnp.concatenate(rows, axis=0).T[64:97]
+    send(embed, embed_out)
+    summed = jnp.sum(group_sums[:, 6:8, :], axis=0)
+    bias[...] = summed[0:1, :64]
+    send(bias, bias_out)
+    frequency[0:1, :] = summed[0:1, 64:]
+    frequency[1:2, :] = summed[1:2, :64]
+    send(frequency, frequency_out)
+    for g in range(8):
+        decay[0:1, 64 * g : 64 * g + 64] = group_sums[g, 7:8, 64:]
+    send(decay, decay_out)
+    for copy in copies:
+        copy.wait()
 
 
 def local(
@@ -363,68 +438,82 @@
 ):
     total = 2 * signal.shape[2]
     scale = 1.0 / math.sqrt(16 * signal.shape[2])
-    both = jnp.stack(
-        [signal.reshape(16, 4, 64, 128), signal_grad.reshape(16, 4, 64, 128)], axis=2
-    )
     factors = [max(1, int(0.45 * total * 10000.0 ** (-band / 16))) for band in range(16)]
     bands = np.repeat(np.array(factors, np.int32)[:, None], 128, axis=1)
     tables = transform_tables(total, scale)
     vmem = pl.BlockSpec(memory_space=pltpu.VMEM)
     f32 = jnp.float32
     lags = pltpu.VMEM((64, 1024), f32)
-    outs = pl.pallas_call(
+    stored = [jnp.asarray(t) for t in tables] + [
+        jnp.asarray(bands),
+        embed_weight.T,
+        embed_bias.reshape(1, 64),
+        hidden_weight,
+        frequency,
+        output_weight.T,
+        decay_rate.reshape(1, 512),
+    ]
+    hbm = pl.BlockSpec(memory_space=pltpu.HBM)
+    landed, pieces, group_sums = pl.pallas_call(
         kernel,
         out_shape=[
-            jax.ShapeDtypeStruct(shape, f32)
-            for shape in [(512, 128), (64, 33), (1, 64), (64, 64), (2, 64), (512, 64), (1, 512)]
+            jax.ShapeDtypeStruct(shape, f32) for shape in [(8, 64, 128), (16, 24, 128), (8, 8, 128)]
         ],
-        in_specs=[pl.BlockSpec(memory_space=pl.ANY)] + [vmem] * 12,
-        out_specs=[vmem] * 7,
+        in_specs=[hbm] * 14,
+        out_specs=[vmem] * 3,
         scratch_shapes=[
+            *[pltpu.VMEM(t.shape, t.dtype) for t in stored],
+            pltpu.VMEM((2, 64, 8192), jnp.bfloat16),
+            pltpu.VMEM((1152, 128), f32),
+            pltpu.VMEM((16, 4, 2, 64, 128), jnp.bfloat16),
             pltpu.VMEM((16, 4, 2, 64, 128), jnp.bfloat16),
             pltpu.VMEM((256, 256), f32),
             pltpu.VMEM((16, 8, 512), f32),
             pltpu.VMEM((16, 8, 512), f32),
             pltpu.VMEM((8, 64, 128), f32),
-            pltpu.VMEM((8, 64, 128), f32),
             pltpu.VMEM((128, 1024), f32),
-            pltpu.VMEM((64, 128), f32),
+            pltpu.VMEM((128, 64), f32),
             pltpu.VMEM((512, 128), f32),
+            pltpu.VMEM((512, 64), f32),
             *[lags] * 8,
             pltpu.VMEM((16, 8, 128), f32),
             pltpu.VMEM((16, 8, 128), f32),
             pltpu.VMEM((8, 128), f32),
-            pltpu.VMEM((8, 8, 128), f32),
             pltpu.VMEM((24, 128), f32),
-            pltpu.VMEM((16, 24, 128), f32),
             pltpu.SemaphoreType.DMA,
+            pltpu.SemaphoreType.DMA((2,)),
+            pltpu.SemaphoreType.DMA((12,)),
             pltpu.SemaphoreType.DMA((4, 15)),
             pltpu.SemaphoreType.DMA((4, 15)),
             pltpu.SemaphoreType.DMA((2, 7)),
             pltpu.SemaphoreType.DMA((2, 7)),
         ],
         compiler_params=pltpu.CompilerParams(
-            collective_id=0, has_side_effects=True, vmem_limit_bytes=40 * 1024 * 1024
+            collective_id=0, has_side_effects=True, vmem_limit_bytes=63 * 1024 * 1024
         ),
-    )(
-        both,
-        *[jnp.asarray(t) for t in tables],
-        jnp.asarray(bands),
-        embed_weight,
-        embed_bias.reshape(1, 64),
-        hidden_weight,
-        frequency,
-        output_weight,
-        decay_rate.reshape(1, 512),
-    )
+    )(signal[0], signal_grad[0], *stored)
+    shapes = [(512, 128), (33, 64), (1, 64), (64, 64), (2, 64), (64, 512), (1, 512)]
+    outs = pl.pallas_call(
+        finish,
+        out_shape=[jax.ShapeDtypeStruct(shape, f32) for shape in shapes],
+        in_specs=[vmem] * 3,
+        out_specs=[hbm] * 7,
+        scratch_shapes=[
+            *[pltpu.VMEM(shape, f32) for shape in shapes[1:5]],
+            pltpu.VMEM((512, 64), f32),
+            *[pltpu.VMEM(shape, f32) for shape in shapes[5:]],
+            pltpu.SemaphoreType.DMA((7,)),
+        ],
+        compiler_params=pltpu.CompilerParams(vmem_limit_bytes=63 * 1024 * 1024),
+    )(landed.reshape(512, 128), pieces, group_sums)
     lag_grad, embed_grad, bias_grad, hidden_grad, frequency_grad, output_grad, decay_grad = outs
     return (
         lag_grad,
-        embed_grad,
+        embed_grad.T,
         bias_grad.reshape(64),
         hidden_grad,
         frequency_grad,
-        output_grad,
+        output_grad.T,
         decay_grad.reshape(512),
     )
 

time: 80.7 us -> 63.6 us (0.79)
  local copies, waits for them, and re-layouts: 17.7 us -> 0 us
  Pallas kernels: 61.4 us -> 62.8 us
    unnamed x47 -> x0, local copies, waits for them, and re-layouts: 17.7 us -> none
    pallas_call x0 -> x1, Pallas kernels: none -> 2.02 us  [local(): pl.pallas_call(finish, out_shape=[jax.ShapeDtypeStruct(shape, f32) for sh...]
where the time goes in v3:
time: 63.6 us; the launch traced here: 63.4 us
  Pallas kernels  62.8 us (99%)
  between operations  0.64 us (1%)
    pallas_call x1, Pallas kernels, local(): pl.pallas_call(kernel, out_shape=[jax.ShapeDtypeStruct(shape, f32) for sh...  60.8 us
    pallas_call x1, Pallas kernels, local(): pl.pallas_call(finish, out_shape=[jax.ShapeDtypeStruct(shape, f32) for sh...  2.02 us

profile of v3, /device:TPU:1, one launch (start us, length us, event | category | flops | bytes accessed | tf_op | source)
XLA Modules:
  0.0 63.4 jit_solution(1462628328639666454)
XLA Ops:
  0.6 60.8 %shard_map.189 = (f32[8,64,128]{2,1,0:T(8,128)}, f32[16,24,128]{2,1,0:T(8,128)}, f32[8,8,128]{2,1,0:T(8,128)}) custom-call(bf16[64,8192]{1,0:T(8,128)(2,1)} %bitcast.11, bf16[64,8192]{1,0:T(8,128)(2,1)} %bitcast.12, bf16[128,128]{1,0:T(8,128)(2,1)} %constant.12.clone.refs_0_, f32[2,64,128]{2,1,0:T(8,128)} %constant.13.clone.refs_1_, ...), custom_call_target="tpu_custom_call" | custom-call | tf_op jit(solution)/shard_map/pallas_call | solution.py:457
  61.4 2.0 %shard_map.190 = (f32[512,128]{1,0:T(8,128)}, f32[33,64]{1,0:T(8,128)}, f32[1,64]{1,0:T(1,128)}, f32[64,64]{1,0:T(8,128)}, f32[2,64]{1,0:T(2,128)}, /*index=5*/f32[64,512]{1,0:T(8,128)}, f32[1,512]{1,0:T(1,128)}) custom-call(f32[512,128]{1,0:T(8,128)} %bitcast.13, f32[16,24,128]{2,1,0:T(8,128)} %get-tuple-element.18.pieces, ...), custom_call_target="tpu_custom_call" | custom-call | tf_op jit(solution)/shard_map/pallas_call | solution.py:496

commit v4 on v3

--- a/solution.py
+++ b/solution.py
@@ -146,6 +146,7 @@
         local_sem,
         input_sem,
         table_sem,
+        arrive_sem,
         dp_send,
         dp_recv,
         chan_send,
@@ -198,30 +199,36 @@
     own.start()
     pl.semaphore_wait(barrier, len(dp_peers) + len(chan_peers))
 
-    def exchange(stage, peers, sends, recvs, source, target, whole=False):
-        copies = []
+    def exchange(peers, send, recvs, source, target, nearest=False):
         order = list(enumerate(peers))
-        for at, (index, where) in order if whole else order[::-1]:
-            copy = pltpu.make_async_remote_copy(
+        for at, (index, where) in order if nearest else order[::-1]:
+            pltpu.make_async_remote_copy(
                 source(index),
                 target(at),
-                sends.at[stage, at],
-                recvs.at[stage, at],
+                send,
+                recvs.at[at] if nearest else recvs,
                 device_id=where,
                 device_id_type=MESH_ID,
-            )
-            copy.start()
-            copies.append(copy)
-        return copies
-
-    over_dp = lambda stage, source, target: exchange(
-        stage, dp_peers, dp_send, dp_recv, source, target, stage == 0
+            ).start()
+
+    def all_bytes(buffer, sem, count):
+        part = buffer.at[pl.ds(0, count)]
+        pltpu.make_async_copy(part, part, sem).wait()
+
+    def over_dp(stage, source, target):
+        exchange(dp_peers, dp_send.at[stage], dp_recv.at[stage], source, target)
+
+    def over_chan(stage, source, target):
+        exchange(chan_peers, chan_send.at[stage], chan_recv.at[stage], source, target)
+
+    exchange(
+        dp_peers,
+        dp_send.at[0],
+        arrive_sem,
+        lambda index: both.at[index],
+        lambda at: arrived.at[at + 1],
+        nearest=True,
     )
-    over_chan = lambda stage, source, target: exchange(
-        stage, chan_peers, chan_send, chan_recv, source, target
-    )
-
-    inputs = over_dp(0, lambda index: both.at[index], lambda at: arrived.at[at + 1])
 
     for fetch in fetches:
         fetch.wait()
@@ -289,8 +296,8 @@
         pltpu.make_async_remote_copy(
             both.at[0],
             arrived.at[at + 1],
-            dp_send.at[0, at],
-            dp_recv.at[0, at],
+            dp_send.at[0],
+            arrive_sem.at[at],
             device_id={"y": y, "x": lax.rem(x + 1, 4)},
             device_id_type=MESH_ID,
         ).wait_recv()
@@ -309,16 +316,16 @@
     result = dot(last[...], jnp.concatenate([high, low, high], axis=0))
     lags[...] = result.reshape(16, 8, 512)
 
-    to_owner = over_dp(1, lambda index: lags.at[index], lambda at: mine.at[me])
+    over_dp(1, lambda index: lags.at[index], lambda at: mine.at[me])
     mine[me] = lags[me]
-    for copy in to_owner:
-        copy.wait_recv()
+    all_bytes(both, dp_send.at[0], 15)
+    all_bytes(mine, dp_recv.at[1], 15)
     for lag_row in range(8):
         for channel in range(4):
             rows[lag_row, pl.ds(channel, 16, stride=4), :] = mine[
                 :, lag_row, 128 * channel : 128 * channel + 128
             ]
-    to_row = over_chan(0, lambda index: rows.at[index], lambda at: landed.at[group])
+    over_chan(0, lambda index: rows.at[index], lambda at: landed.at[group])
     landed[group] = rows[group]
 
     lanes = ((1,), (1,))
@@ -348,26 +355,27 @@
     partial[:, 6, :] = jnp.broadcast_to(vectors, (16, 128))
     vectors = jnp.concatenate([frequency_second[:1], decay_row[:1]], axis=1)
     partial[:, 7, :] = jnp.broadcast_to(vectors, (16, 128))
-    to_sum = over_dp(2, lambda index: partial.at[index], lambda at: partials.at[me])
+    over_dp(2, lambda index: partial.at[index], lambda at: partials.at[me])
     partials[me] = partial[me]
-    for copy in to_sum:
-        copy.wait_recv()
+    all_bytes(lags, dp_send.at[1], 15)
+    all_bytes(rows, chan_send.at[0], 7)
+    all_bytes(partials, dp_recv.at[2], 15)
     own_sum[...] = jnp.sum(partials[...], axis=0)
-    to_groups = over_chan(1, lambda index: own_sum, lambda at: group_sums.at[group])
+    over_chan(1, lambda index: own_sum, lambda at: group_sums.at[group])
     group_sums[group] = own_sum[...]
-    for copy in to_groups:
-        copy.wait_recv()
+    all_bytes(group_sums, chan_recv.at[1], 7)
     summed = jnp.sum(group_sums[...], axis=0)
     piece[0:4, :] = summed[0:4]
     piece[20:24, :] = jnp.zeros((4, 128), jnp.float32)
     for g in range(8):
         piece[4 + 2 * g : 6 + 2 * g, :] = group_sums[g, 4:6, :]
-    to_all = over_dp(3, lambda index: piece, lambda at: pieces.at[me])
+    over_dp(3, lambda index: piece, lambda at: pieces.at[me])
     pieces[me] = piece[...]
-    for copy in to_row + to_all:
-        copy.wait_recv()
-    for copy in inputs + to_owner + to_row + to_sum + to_groups + to_all:
-        copy.wait_send()
+    all_bytes(landed, chan_recv.at[0], 7)
+    all_bytes(pieces, dp_recv.at[3], 15)
+    all_bytes(partial, dp_send.at[2], 15)
+    all_bytes(group_sums, chan_send.at[1], 7)
+    all_bytes(pieces, dp_send.at[3], 15)
 
 
 def finish(
@@ -483,15 +491,16 @@
             pltpu.SemaphoreType.DMA,
             pltpu.SemaphoreType.DMA((2,)),
             pltpu.SemaphoreType.DMA((12,)),
-            pltpu.SemaphoreType.DMA((4, 15)),
-            pltpu.SemaphoreType.DMA((4, 15)),
-            pltpu.SemaphoreType.DMA((2, 7)),
-            pltpu.SemaphoreType.DMA((2, 7)),
+            pltpu.SemaphoreType.DMA((15,)),
+            pltpu.SemaphoreType.DMA((4,)),
+            pltpu.SemaphoreType.DMA((4,)),
+            pltpu.SemaphoreType.DMA((2,)),
+            pltpu.SemaphoreType.DMA((2,)),
         ],
         compiler_params=pltpu.CompilerParams(
-            collective_id=0, has_side_effects=True, vmem_limit_bytes=63 * 1024 * 1024
+            collective_id=0, has_side_effects=True, vmem_limit_bytes=40 * 1024 * 1024
         ),
-    )(signal[0], signal_grad[0], *stored)
+    )(*[pltpu.with_memory_space_constraint(t, pltpu.HBM) for t in (signal[0], signal_grad[0], *stored)])
     shapes = [(512, 128), (33, 64), (1, 64), (64, 64), (2, 64), (64, 512), (1, 512)]
     outs = pl.pallas_call(
         finish,
@@ -504,7 +513,7 @@
             *[pltpu.VMEM(shape, f32) for shape in shapes[5:]],
             pltpu.SemaphoreType.DMA((7,)),
         ],
-        compiler_params=pltpu.CompilerParams(vmem_limit_bytes=63 * 1024 * 1024),
+        compiler_params=pltpu.CompilerParams(vmem_limit_bytes=8 * 1024 * 1024),
     )(landed.reshape(512, 128), pieces, group_sums)
     lag_grad, embed_grad, bias_grad, hidden_grad, frequency_grad, output_grad, decay_grad = outs
     return (

time: 63.6 us -> 60.5 us (0.951)
  Pallas kernels: 62.8 us -> 59.7 us
    pallas_call x1, Pallas kernels: 60.8 us -> 58.7 us  [local(): pl.pallas_call(kernel, out_shape=[jax.ShapeDtypeStruct(shape, f32) for sh...]
    pallas_call x1, Pallas kernels: 2.02 us -> 0.96 us  [local(): pl.pallas_call(finish, out_shape=[jax.ShapeDtypeStruct(shape, f32) for sh...]
where the time goes in v4:
time: 60.5 us; the launch traced here: 60.3 us
  Pallas kernels  59.7 us (99%)
  between operations  0.64 us (1%)
    pallas_call x1, Pallas kernels, local(): pl.pallas_call(kernel, out_shape=[jax.ShapeDtypeStruct(shape, f32) for sh...  58.7 us

profile of v4, /device:TPU:1, one launch (start us, length us, event | category | flops | bytes accessed | tf_op | source)
XLA Modules:
  0.0 60.3 jit_solution(17970319611897062762)
XLA Ops:
  0.6 58.7 %shard_map.189 = (f32[8,64,128]{2,1,0:T(8,128)S(1)}, f32[16,24,128]{2,1,0:T(8,128)S(1)}, f32[8,8,128]{2,1,0:T(8,128)S(1)}) custom-call(bf16[64,8192]{1,0:T(8,128)(2,1)} %bitcast.12, bf16[64,8192]{1,0:T(8,128)(2,1)} %bitcast.13, bf16[128,128]{1,0:T(8,128)(2,1)} %constant.12.clone.refs_0_, f32[2,64,128]{2,1,0:T(8,128)} %constant.13.clone.refs_1_, ...), custom_call_target="tpu_custom_call" | custom-call | tf_op jit(solution)/shard_map/pallas_call | solution.py:465
  59.4 1.0 %shard_map.190 = (f32[512,128]{1,0:T(8,128)}, f32[33,64]{1,0:T(8,128)}, f32[1,64]{1,0:T(1,128)}, f32[64,64]{1,0:T(8,128)}, f32[2,64]{1,0:T(2,128)}, /*index=5*/f32[64,512]{1,0:T(8,128)}, f32[1,512]{1,0:T(1,128)}) custom-call(f32[512,128]{1,0:T(8,128)S(1)} %bitcast.11, f32[16,24,128]{2,1,0:T(8,128)S(1)} %get-tuple-element.18.pieces, ...), custom_call_target="tpu_custom_call" | custom-call | tf_op jit(solution)/shard_map/pallas_call | solution.py:505

commit v5 on v4

--- a/solution.py
+++ b/solution.py
@@ -146,6 +146,7 @@
         local_sem,
         input_sem,
         table_sem,
+        entered,
         arrive_sem,
         dp_send,
         dp_recv,
@@ -166,8 +167,13 @@
     for dz, dc in PEERS[1:]:
         tz, tc = lax.rem(z + dz, 4), lax.rem(core + dc, 2)
         chan_peers.append((tz * 2 + tc, {"z": tz, "core": tc}))
-    for _, where in dp_peers[::-1] + chan_peers[::-1]:
-        pl.semaphore_signal(barrier, 1, device_id=where, device_id_type=MESH_ID)
+    neighbours = [where for _, where in dp_peers[:4] + chan_peers[:3]]
+
+    def greet(sem):
+        for where in neighbours:
+            pl.semaphore_signal(sem, 1, device_id=where, device_id_type=MESH_ID)
+
+    greet(barrier)
     loads = []
     for part, source in enumerate((signal, signal_grad)):
         loads.append(pltpu.make_async_copy(source, natural.at[part], input_sem.at[part]))
@@ -180,6 +186,9 @@
 
     for part in range(2):
         loads[part].wait()
+        if part == 1:
+            pl.semaphore_wait(barrier, 7)
+            greet(entered.at[0])
 
         @pl.loop(0, 4)
         def _(block):
@@ -197,10 +206,9 @@
 
     own = pltpu.make_async_copy(both.at[me], arrived.at[0], local_sem)
     own.start()
-    pl.semaphore_wait(barrier, len(dp_peers) + len(chan_peers))
 
     def exchange(peers, send, recvs, source, target, nearest=False):
-        order = list(enumerate(peers))
+        order = peers if nearest else list(enumerate(peers))
         for at, (index, where) in order if nearest else order[::-1]:
             pltpu.make_async_remote_copy(
                 source(index),
@@ -221,15 +229,17 @@
     def over_chan(stage, source, target):
         exchange(chan_peers, chan_send.at[stage], chan_recv.at[stage], source, target)
 
-    exchange(
-        dp_peers,
-        dp_send.at[0],
-        arrive_sem,
-        lambda index: both.at[index],
-        lambda at: arrived.at[at + 1],
-        nearest=True,
-    )
-
+    def send_inputs(first_peer, last_peer):
+        exchange(
+            list(enumerate(dp_peers))[first_peer:last_peer],
+            dp_send.at[0],
+            arrive_sem,
+            lambda index: both.at[index],
+            lambda at: arrived.at[at + 1],
+            nearest=True,
+        )
+
+    send_inputs(0, 4)
     for fetch in fetches:
         fetch.wait()
 
@@ -243,6 +253,9 @@
     table[0:1, :] = lag[:1].astype(jnp.float32) * (1.0 / 8192)
     table[1:17, :] = sines
     table[17:33, :] = cosines
+    pl.semaphore_wait(entered.at[0], 7)
+    greet(entered.at[1])
+    send_inputs(4, 10)
     wide = lambda columns: jnp.concatenate([columns] * 8, axis=1)
     bias = as_columns(jnp.concatenate([embed_bias[...]] * 2, axis=1))[:64]
     freq_rows = jnp.concatenate([frequency[...]] * 2, axis=1)
@@ -252,6 +265,9 @@
     sine, cosine = sine_cosine(wide(freq_first) * before)
     sine_first[...] = sine
     cosine_first[...] = cosine
+    pl.semaphore_wait(entered.at[1], 7)
+    greet(entered.at[2])
+    send_inputs(10, 14)
     before = exact_dot(hidden_weight[...], sine)
     pre_second[...] = before
     sine, cosine = sine_cosine(wide(freq_second) * before)
@@ -288,6 +304,8 @@
         spectrum[:, :128] += in_real * grad_real + in_imag * grad_imag
         spectrum[:, 128:] += in_real * grad_imag - in_imag * grad_real
 
+    pl.semaphore_wait(entered.at[2], 7)
+    send_inputs(14, 15)
     own.wait()
     add_sequence(0)
 
@@ -491,6 +509,7 @@
             pltpu.SemaphoreType.DMA,
             pltpu.SemaphoreType.DMA((2,)),
             pltpu.SemaphoreType.DMA((12,)),
+            pltpu.SemaphoreType.REGULAR((3,)),
             pltpu.SemaphoreType.DMA((15,)),
             pltpu.SemaphoreType.DMA((4,)),
             pltpu.SemaphoreType.DMA((4,)),

time: 60.5 us -> 59.3 us (0.980)
  Pallas kernels: 59.7 us -> 58.5 us
    pallas_call x1, Pallas kernels: 58.7 us -> 57.6 us  [local(): pl.pallas_call(kernel, out_shape=[jax.ShapeDtypeStruct(shape, f32) for sh...]
where the time goes in v5:
time: 59.3 us; the launch traced here: 59.2 us
  Pallas kernels  58.5 us (99%)
  between operations  0.64 us (1%)
    pallas_call x1, Pallas kernels, local(): pl.pallas_call(kernel, out_shape=[jax.ShapeDtypeStruct(shape, f32) for sh...  57.6 us

profile of v5, /device:TPU:1, one launch (start us, length us, event | category | flops | bytes accessed | tf_op | source)
XLA Modules:
  0.0 59.2 jit_solution(4059520682768284118)
XLA Ops:
  0.6 57.6 %shard_map.189 = (f32[8,64,128]{2,1,0:T(8,128)S(1)}, f32[16,24,128]{2,1,0:T(8,128)S(1)}, f32[8,8,128]{2,1,0:T(8,128)S(1)}) custom-call(bf16[64,8192]{1,0:T(8,128)(2,1)} %bitcast.12, bf16[64,8192]{1,0:T(8,128)(2,1)} %bitcast.13, bf16[128,128]{1,0:T(8,128)(2,1)} %constant.12.clone.refs_0_, f32[2,64,128]{2,1,0:T(8,128)} %constant.13.clone.refs_1_, ...), custom_call_target="tpu_custom_call" | custom-call | tf_op jit(solution)/shard_map/pallas_call | solution.py:483
  58.2 1.0 %shard_map.190 = (f32[512,128]{1,0:T(8,128)}, f32[33,64]{1,0:T(8,128)}, f32[1,64]{1,0:T(1,128)}, f32[64,64]{1,0:T(8,128)}, f32[2,64]{1,0:T(2,128)}, /*index=5*/f32[64,512]{1,0:T(8,128)}, f32[1,512]{1,0:T(1,128)}) custom-call(f32[512,128]{1,0:T(8,128)S(1)} %bitcast.11, f32[16,24,128]{2,1,0:T(8,128)S(1)} %get-tuple-element.18.pieces, ...), custom_call_target="tpu_custom_call" | custom-call | tf_op jit(solution)/shard_map/pallas_call | solution.py:524

commit v6 on v5

--- a/solution.py
+++ b/solution.py
@@ -66,6 +66,19 @@
     return jnp.dot(a, b, preferred_element_type=jnp.float32)
 
 
+def lane_dot(a, b):
+    return lax.dot_general(a, b, (((1,), (1,)), ((), ())), preferred_element_type=jnp.float32)
+
+
+def kept(values):
+    high, low = split_values(values)
+    return jnp.concatenate([high, high, low], axis=1)
+
+
+def met(high, low, axis):
+    return jnp.concatenate([high, low, high], axis=axis)
+
+
 def exact_dot(a, b, dims=((1,), (0,))):
     return lax.dot_general(
         a, b, (dims, ((), ())), precision=lax.Precision.HIGHEST, preferred_element_type=jnp.float32
@@ -107,6 +120,7 @@
         landed,
         pieces,
         group_sums,
+        used,
         first,
         twist,
         forward,
@@ -128,13 +142,14 @@
         mine,
         rows,
         table,
+        table_kept,
+        weights_kept,
+        hidden_kept,
         embed_pad,
         decay_columns,
         output_rows,
-        pre_first,
         sine_first,
         cosine_first,
-        pre_second,
         sine_second,
         cosine_second,
         window,
@@ -180,7 +195,7 @@
         loads[-1].start()
     fetches = []
     for at, source in enumerate(stored):
-        fetches.append(pltpu.make_async_copy(source, refs[15 + at], table_sem.at[at]))
+        fetches.append(pltpu.make_async_copy(source, refs[16 + at], table_sem.at[at]))
         fetches[-1].start()
     spectrum[...] = jnp.zeros_like(spectrum)
 
@@ -246,6 +261,8 @@
     table[...] = jnp.zeros_like(table)
     embed_pad[...] = jnp.zeros_like(embed_pad)
     embed_pad[:33, :] = embed_weight[...]
+    embed_pad[33:34, :] = embed_bias[...]
+    table[33:34, :] = jnp.ones((1, 1024), jnp.float32)
     position = me * 1024 + lax.broadcasted_iota(jnp.int32, (16, 1024), 1)
     lag = jnp.where(me < 8, position, position - 16384)
     phase = ((lag * jnp.concatenate([bands[...]] * 8, axis=1)) & 16383).astype(jnp.float32)
@@ -257,26 +274,29 @@
     greet(entered.at[1])
     send_inputs(4, 10)
     wide = lambda columns: jnp.concatenate([columns] * 8, axis=1)
-    bias = as_columns(jnp.concatenate([embed_bias[...]] * 2, axis=1))[:64]
     freq_rows = jnp.concatenate([frequency[...]] * 2, axis=1)
     freq_first, freq_second = as_columns(freq_rows[0:1])[:64], as_columns(freq_rows[1:2])[:64]
-    before = exact_dot(embed_pad[...], table[...], ((0,), (0,))) + wide(bias)
-    pre_first[...] = before
-    sine, cosine = sine_cosine(wide(freq_first) * before)
-    sine_first[...] = sine
+    sine, cosine = sine_cosine(
+        wide(freq_first) * exact_dot(embed_pad[...], table[...], ((0,), (0,)))
+    )
+    table_kept[...] = kept(table[...])
+    sine_first[...] = kept(sine)
     cosine_first[...] = cosine
     pl.semaphore_wait(entered.at[1], 7)
     greet(entered.at[2])
     send_inputs(10, 14)
-    before = exact_dot(hidden_weight[...], sine)
-    pre_second[...] = before
-    sine, cosine = sine_cosine(wide(freq_second) * before)
-    sine_second[...] = sine
+    sine, cosine = sine_cosine(wide(freq_second) * exact_dot(hidden_weight[...], sine))
+    sine_second[...] = kept(sine)
     cosine_second[...] = cosine
+    used[0:64, :] = embed_pad[...]
+    used[64:128, :] = hidden_weight[...].T
+    used[128:130, :] = frequency[...]
+    hidden_kept[...] = kept((hidden_weight[...] * freq_second[:, :64]).T)
     decay_columns[...] = as_columns(decay_rate[...])
     output_rows[...] = output_weight[...].T
     weights = output_rows[pl.ds(pl.multiple_of(group * 64, 64), 64), :]
     decay = decay_columns[pl.ds(pl.multiple_of(group * 64, 64), 64), :]
+    weights_kept[...] = kept(weights.T)
     distance = jnp.abs(lag[:1]).astype(jnp.float32) * (1.0 / 8192)
     shape = jnp.exp(-wide(decay) * distance) * (1.0 / 128)
     window[...] = shape
@@ -346,33 +366,28 @@
     over_chan(0, lambda index: rows.at[index], lambda at: landed.at[group])
     landed[group] = rows[group]
 
-    lanes = ((1,), (1,))
-    down = ((0,), (0,))
-    ones = jnp.ones((8, 1024), jnp.float32)
     grad = jnp.concatenate([rows[lag_row] for lag_row in range(8)], axis=1)
-    decay_row = exact_dot(ones, grad * slope[...], lanes)
-    shaped = grad * window[...]
-    output_grad = exact_dot(shaped, sine_second[...], lanes)
-    turned = exact_dot(weights, shaped, down) * cosine_second[...]
-    frequency_second = exact_dot(ones, turned * pre_second[...], lanes)
-    turned = turned * wide(freq_second)
-    hidden_grad = exact_dot(turned, sine_first[...], lanes)
-    turned = exact_dot(hidden_weight[...], turned, down) * cosine_first[...]
-    frequency_first = exact_dot(ones, turned * pre_first[...], lanes)
-    turned = turned * wide(freq_first)
-    bias_row = exact_dot(ones, turned, lanes)
-    embed_grad = exact_dot(turned, table[...], lanes)
-
-    shared = jnp.concatenate([hidden_grad, embed_grad[:, :64]], axis=1)
+    high, low = split_values(grad * window[...])
+    turned = dot(weights_kept[...], met(high, low, 0)) * cosine_second[...]
+    high_second, low_second = split_values(turned)
+    turned = dot(hidden_kept[...], met(high_second, low_second, 0)) * cosine_first[...]
+    output_grad = lane_dot(met(high, low, 1), sine_second[...])
+    hidden_grad = lane_dot(sine_first[...], met(high_second, low_second, 1))
+    high, low = split_values(grad * slope[...])
+    ones = jnp.ones((8, 2048), jnp.bfloat16)
+    decay_row = lane_dot(ones, jnp.concatenate([high, low], axis=1))
+    high, low = split_values(turned)
+    embed_grad = lane_dot(table_kept[...], met(high, low, 1))
+
+    shared = jnp.concatenate([hidden_grad, embed_grad], axis=1)
     for k in range(4):
         partial[:, k, :] = shared[16 * k : 16 * k + 16]
     packed = jnp.concatenate([output_grad[:32], output_grad[32:]], axis=1)
     for k in range(2):
         partial[:, 4 + k, :] = packed[16 * k : 16 * k + 16]
-    vectors = jnp.concatenate([bias_row[:1], frequency_first[:1]], axis=1)
-    partial[:, 6, :] = jnp.broadcast_to(vectors, (16, 128))
-    vectors = jnp.concatenate([frequency_second[:1], decay_row[:1]], axis=1)
-    partial[:, 7, :] = jnp.broadcast_to(vectors, (16, 128))
+    decays = jnp.concatenate([decay_row[:1], jnp.zeros((1, 64), jnp.float32)], axis=1)
+    partial[:, 6, :] = jnp.broadcast_to(decays, (16, 128))
+    partial[:, 7, :] = jnp.zeros((16, 128), jnp.float32)
     over_dp(2, lambda index: partial.at[index], lambda at: partials.at[me])
     partials[me] = partial[me]
     all_bytes(lags, dp_send.at[1], 15)
@@ -400,6 +415,7 @@
     landed,
     pieces,
     group_sums,
+    used,
     filter_out,
     embed_out,
     bias_out,
@@ -431,22 +447,20 @@
             output_rows[at + 32 : at + 48, :] = block[:, 64:]
     output[...] = output_rows[...].T
     send(output, output_out)
-    rows = []
-    for k in range(4):
-        block = pieces[:, k, :]
-        hidden[16 * k : 16 * k + 16, :] = block[:, :64]
-        rows.append(block)
+    shared = jnp.concatenate([pieces[:, k, :] for k in range(4)], axis=0)
+    scales = jnp.concatenate([used[129:130, :], used[128:129, :]], axis=1)
+    scaled = shared * scales
+    embed[...] = scaled[:33, 64:]
+    send(embed, embed_out)
+    bias[...] = scaled[33:34, 64:]
+    send(bias, bias_out)
+    hidden[...] = scaled.T[:64]
     send(hidden, hidden_out)
-    embed[...] = jnp.concatenate(rows, axis=0).T[64:97]
-    send(embed, embed_out)
-    summed = jnp.sum(group_sums[:, 6:8, :], axis=0)
-    bias[...] = summed[0:1, :64]
-    send(bias, bias_out)
-    frequency[0:1, :] = summed[0:1, 64:]
-    frequency[1:2, :] = summed[1:2, :64]
+    frequency[0:1, :] = jnp.sum(shared[:, 64:] * used[0:64, :], axis=0, keepdims=True)
+    frequency[1:2, :] = jnp.sum(shared[:, :64] * used[64:128, :], axis=0, keepdims=True)
     send(frequency, frequency_out)
     for g in range(8):
-        decay[0:1, 64 * g : 64 * g + 64] = group_sums[g, 7:8, 64:]
+        decay[0:1, 64 * g : 64 * g + 64] = group_sums[g, 6:7, :64]
     send(decay, decay_out)
     for copy in copies:
         copy.wait()
@@ -470,6 +484,7 @@
     vmem = pl.BlockSpec(memory_space=pltpu.VMEM)
     f32 = jnp.float32
     lags = pltpu.VMEM((64, 1024), f32)
+    halves = pltpu.VMEM((64, 3072), jnp.bfloat16)
     stored = [jnp.asarray(t) for t in tables] + [
         jnp.asarray(bands),
         embed_weight.T,
@@ -480,13 +495,13 @@
         decay_rate.reshape(1, 512),
     ]
     hbm = pl.BlockSpec(memory_space=pltpu.HBM)
-    landed, pieces, group_sums = pl.pallas_call(
+    landed, pieces, group_sums, used = pl.pallas_call(
         kernel,
         out_shape=[
-            jax.ShapeDtypeStruct(shape, f32) for shape in [(8, 64, 128), (16, 24, 128), (8, 8, 128)]
+            jax.ShapeDtypeStruct(shape, f32) for shape in [(8, 64, 128), (16, 24, 128), (8, 8, 128), (136, 64)]
         ],
         in_specs=[hbm] * 14,
-        out_specs=[vmem] * 3,
+        out_specs=[vmem] * 4,
         scratch_shapes=[
             *[pltpu.VMEM(t.shape, t.dtype) for t in stored],
             pltpu.VMEM((2, 64, 8192), jnp.bfloat16),
@@ -497,11 +512,17 @@
             pltpu.VMEM((16, 8, 512), f32),
             pltpu.VMEM((16, 8, 512), f32),
             pltpu.VMEM((8, 64, 128), f32),
-            pltpu.VMEM((128, 1024), f32),
-            pltpu.VMEM((128, 64), f32),
+            lags,
+            halves,
+            pltpu.VMEM((64, 192), jnp.bfloat16),
+            pltpu.VMEM((64, 192), jnp.bfloat16),
+            pltpu.VMEM((64, 64), f32),
             pltpu.VMEM((512, 128), f32),
             pltpu.VMEM((512, 64), f32),
-            *[lags] * 8,
+            halves,
+            lags,
+            halves,
+            *[lags] * 3,
             pltpu.VMEM((16, 8, 128), f32),
             pltpu.VMEM((16, 8, 128), f32),
             pltpu.VMEM((8, 128), f32),
@@ -524,7 +545,7 @@
     outs = pl.pallas_call(
         finish,
         out_shape=[jax.ShapeDtypeStruct(shape, f32) for shape in shapes],
-        in_specs=[vmem] * 3,
+        in_specs=[vmem] * 4,
         out_specs=[hbm] * 7,
         scratch_shapes=[
             *[pltpu.VMEM(shape, f32) for shape in shapes[1:5]],
@@ -533,7 +554,7 @@
             pltpu.SemaphoreType.DMA((7,)),
         ],
         compiler_params=pltpu.CompilerParams(vmem_limit_bytes=8 * 1024 * 1024),
-    )(landed.reshape(512, 128), pieces, group_sums)
+    )(landed.reshape(512, 128), pieces, group_sums, used)
     lag_grad, embed_grad, bias_grad, hidden_grad, frequency_grad, output_grad, decay_grad = outs
     return (
         lag_grad,

time: 59.3 us -> 57.7 us (0.973)
  Pallas kernels: 58.5 us -> 57 us
    pallas_call x1, Pallas kernels: 57.6 us -> 55.9 us  [local(): pl.pallas_call(kernel, out_shape=[jax.ShapeDtypeStruct(shape, f32) for sh...]
where the time goes in v6:
time: 57.7 us; the launch traced here: 57.6 us
  Pallas kernels  57 us (99%)
  between operations  0.64 us (1%)
    pallas_call x1, Pallas kernels, local(): pl.pallas_call(kernel, out_shape=[jax.ShapeDtypeStruct(shape, f32) for sh...  55.9 us

profile of v6, /device:TPU:1, one launch (start us, length us, event | category | flops | bytes accessed | tf_op | source)
XLA Modules:
  0.0 57.6 jit_solution(3443715744277748355)
XLA Ops:
  0.6 55.9 %shard_map.189 = (f32[8,64,128]{2,1,0:T(8,128)S(1)}, f32[16,24,128]{2,1,0:T(8,128)S(1)}, f32[8,8,128]{2,1,0:T(8,128)S(1)}, f32[136,64]{1,0:T(8,128)S(1)}) custom-call(bf16[64,8192]{1,0:T(8,128)(2,1)} %bitcast.12, bf16[64,8192]{1,0:T(8,128)(2,1)} %bitcast.13, bf16[128,128]{1,0:T(8,128)(2,1)} %constant.12.clone.refs_0_, f32[2,64,128]{2,1,0:T(8,128)} %constant.13.clone.refs_1_, ...), custom_call_target="tpu_custom_call" | custom-call | tf_op jit(solution)/shard_map/pallas_call | solution.py:498
  56.6 1.0 %shard_map.190 = (f32[512,128]{1,0:T(8,128)}, f32[33,64]{1,0:T(8,128)}, f32[1,64]{1,0:T(1,128)}, f32[64,64]{1,0:T(8,128)}, f32[2,64]{1,0:T(2,128)}, /*index=5*/f32[64,512]{1,0:T(8,128)}, f32[1,512]{1,0:T(1,128)}) custom-call(f32[512,128]{1,0:T(8,128)S(1)} %bitcast.11, f32[16,24,128]{2,1,0:T(8,128)S(1)} %get-tuple-element.19.pieces, ...), custom_call_target="tpu_custom_call" | custom-call | tf_op jit(solution)/shard_map/pallas_call | solution.py:545

commit v7 on v6

--- a/solution.py
+++ b/solution.py
@@ -189,38 +189,23 @@
             pl.semaphore_signal(sem, 1, device_id=where, device_id_type=MESH_ID)
 
     greet(barrier)
+    blocks = [lax.rem(y + step, 4) for step in (0, 1, 3, 2)]
     loads = []
-    for part, source in enumerate((signal, signal_grad)):
-        loads.append(pltpu.make_async_copy(source, natural.at[part], input_sem.at[part]))
-        loads[-1].start()
+    for at, block in enumerate(blocks):
+        some = pl.ds(pl.multiple_of(block * 16, 16), 16)
+        for part, source in enumerate((signal, signal_grad)):
+            loads.append(
+                pltpu.make_async_copy(
+                    source.at[some], natural.at[part, at], input_sem.at[2 * at + part]
+                )
+            )
+            loads[-1].start()
     fetches = []
     for at, source in enumerate(stored):
         fetches.append(pltpu.make_async_copy(source, refs[16 + at], table_sem.at[at]))
         fetches[-1].start()
     spectrum[...] = jnp.zeros_like(spectrum)
-
-    for part in range(2):
-        loads[part].wait()
-        if part == 1:
-            pl.semaphore_wait(barrier, 7)
-            greet(entered.at[0])
-
-        @pl.loop(0, 4)
-        def _(block):
-            for tile in range(64):
-                piece_of = natural[
-                    part, pl.ds(pl.multiple_of(block * 16, 16), 16), 128 * tile : 128 * tile + 128
-                ]
-                spread[pl.ds(tile, 16, stride=72), :] = piece_of.astype(jnp.float32)
-            for peer in range(4):
-                for channel in range(4):
-                    at = 72 * (4 * peer + channel)
-                    both[4 * block + peer, channel, part] = spread[at : at + 64, :].astype(
-                        jnp.bfloat16
-                    )
-
-    own = pltpu.make_async_copy(both.at[me], arrived.at[0], local_sem)
-    own.start()
+    partial[:, 7, :] = jnp.zeros((16, 128), jnp.float32)
 
     def exchange(peers, send, recvs, source, target, nearest=False):
         order = peers if nearest else list(enumerate(peers))
@@ -244,9 +229,10 @@
     def over_chan(stage, source, target):
         exchange(chan_peers, chan_send.at[stage], chan_recv.at[stage], source, target)
 
-    def send_inputs(first_peer, last_peer):
+    def send_inputs(*offsets):
+        ranks = [OFFSETS.index(offset) - 1 for offset in offsets]
         exchange(
-            list(enumerate(dp_peers))[first_peer:last_peer],
+            [(rank, dp_peers[rank]) for rank in ranks],
             dp_send.at[0],
             arrive_sem,
             lambda index: both.at[index],
@@ -254,7 +240,34 @@
             nearest=True,
         )
 
-    send_inputs(0, 4)
+    def lay_out(at):
+        for part in range(2):
+            loads[2 * at + part].wait()
+            for tile in range(64):
+                some = natural[part, at, :, 128 * tile : 128 * tile + 128]
+                spread[part, pl.ds(tile, 16, stride=72), :] = some.astype(jnp.float32)
+            for peer in range(4):
+                for channel in range(4):
+                    row = 72 * (4 * peer + channel)
+                    both[4 * blocks[at] + peer, channel, part] = spread[
+                        part, row : row + 64, :
+                    ].astype(jnp.bfloat16)
+
+    lay_out(0)
+    pl.semaphore_wait(barrier, 7)
+    greet(entered.at[0])
+    send_inputs((0, 1), (0, 3))
+    lay_out(1)
+    send_inputs((1, 0))
+    lay_out(2)
+    send_inputs((3, 0))
+    pl.semaphore_wait(entered.at[0], 7)
+    greet(entered.at[1])
+    lay_out(3)
+    own = pltpu.make_async_copy(both.at[me], arrived.at[0], local_sem)
+    own.start()
+    send_inputs((0, 2), (1, 1), (1, 3), (2, 0), (3, 1), (3, 3))
+
     for fetch in fetches:
         fetch.wait()
 
@@ -270,9 +283,6 @@
     table[0:1, :] = lag[:1].astype(jnp.float32) * (1.0 / 8192)
     table[1:17, :] = sines
     table[17:33, :] = cosines
-    pl.semaphore_wait(entered.at[0], 7)
-    greet(entered.at[1])
-    send_inputs(4, 10)
     wide = lambda columns: jnp.concatenate([columns] * 8, axis=1)
     freq_rows = jnp.concatenate([frequency[...]] * 2, axis=1)
     freq_first, freq_second = as_columns(freq_rows[0:1])[:64], as_columns(freq_rows[1:2])[:64]
@@ -284,7 +294,7 @@
     cosine_first[...] = cosine
     pl.semaphore_wait(entered.at[1], 7)
     greet(entered.at[2])
-    send_inputs(10, 14)
+    send_inputs((1, 2), (2, 1), (2, 3), (3, 2))
     sine, cosine = sine_cosine(wide(freq_second) * exact_dot(hidden_weight[...], sine))
     sine_second[...] = kept(sine)
     cosine_second[...] = cosine
@@ -325,7 +335,7 @@
         spectrum[:, 128:] += in_real * grad_imag - in_imag * grad_real
 
     pl.semaphore_wait(entered.at[2], 7)
-    send_inputs(14, 15)
+    send_inputs((2, 2))
     own.wait()
     add_sequence(0)
 
@@ -363,8 +373,6 @@
             rows[lag_row, pl.ds(channel, 16, stride=4), :] = mine[
                 :, lag_row, 128 * channel : 128 * channel + 128
             ]
-    over_chan(0, lambda index: rows.at[index], lambda at: landed.at[group])
-    landed[group] = rows[group]
 
     grad = jnp.concatenate([rows[lag_row] for lag_row in range(8)], axis=1)
     high, low = split_values(grad * window[...])
@@ -387,9 +395,10 @@
         partial[:, 4 + k, :] = packed[16 * k : 16 * k + 16]
     decays = jnp.concatenate([decay_row[:1], jnp.zeros((1, 64), jnp.float32)], axis=1)
     partial[:, 6, :] = jnp.broadcast_to(decays, (16, 128))
-    partial[:, 7, :] = jnp.zeros((16, 128), jnp.float32)
     over_dp(2, lambda index: partial.at[index], lambda at: partials.at[me])
     partials[me] = partial[me]
+    over_chan(0, lambda index: rows.at[index], lambda at: landed.at[group])
+    landed[group] = rows[group]
     all_bytes(lags, dp_send.at[1], 15)
     all_bytes(rows, chan_send.at[0], 7)
     all_bytes(partials, dp_recv.at[2], 15)
@@ -399,7 +408,6 @@
     all_bytes(group_sums, chan_recv.at[1], 7)
     summed = jnp.sum(group_sums[...], axis=0)
     piece[0:4, :] = summed[0:4]
-    piece[20:24, :] = jnp.zeros((4, 128), jnp.float32)
     for g in range(8):
         piece[4 + 2 * g : 6 + 2 * g, :] = group_sums[g, 4:6, :]
     over_dp(3, lambda index: piece, lambda at: pieces.at[me])
@@ -498,14 +506,14 @@
     landed, pieces, group_sums, used = pl.pallas_call(
         kernel,
         out_shape=[
-            jax.ShapeDtypeStruct(shape, f32) for shape in [(8, 64, 128), (16, 24, 128), (8, 8, 128), (136, 64)]
+            jax.ShapeDtypeStruct(shape, f32) for shape in [(8, 64, 128), (16, 20, 128), (8, 8, 128), (136, 64)]
         ],
         in_specs=[hbm] * 14,
         out_specs=[vmem] * 4,
         scratch_shapes=[
             *[pltpu.VMEM(t.shape, t.dtype) for t in stored],
-            pltpu.VMEM((2, 64, 8192), jnp.bfloat16),
-            pltpu.VMEM((1152, 128), f32),
+            pltpu.VMEM((2, 4, 16, 8192), jnp.bfloat16),
+            pltpu.VMEM((2, 1152, 128), f32),
             pltpu.VMEM((16, 4, 2, 64, 128), jnp.bfloat16),
             pltpu.VMEM((16, 4, 2, 64, 128), jnp.bfloat16),
             pltpu.VMEM((256, 256), f32),
@@ -526,9 +534,9 @@
             pltpu.VMEM((16, 8, 128), f32),
             pltpu.VMEM((16, 8, 128), f32),
             pltpu.VMEM((8, 128), f32),
-            pltpu.VMEM((24, 128), f32),
+            pltpu.VMEM((20, 128), f32),
             pltpu.SemaphoreType.DMA,
-            pltpu.SemaphoreType.DMA((2,)),
+            pltpu.SemaphoreType.DMA((8,)),
             pltpu.SemaphoreType.DMA((12,)),
             pltpu.SemaphoreType.REGULAR((3,)),
             pltpu.SemaphoreType.DMA((15,)),

time: 57.7 us -> 56.7 us (0.983)
  Pallas kernels: 57 us -> 56 us
    pallas_call x1, Pallas kernels: 55.9 us -> 54.9 us  [local(): pl.pallas_call(kernel, out_shape=[jax.ShapeDtypeStruct(shape, f32) for sh...]
where the time goes in v7:
time: 56.7 us; the launch traced here: 56.6 us
  Pallas kernels  56 us (99%)
  between operations  0.64 us (1%)
    pallas_call x1, Pallas kernels, local(): pl.pallas_call(kernel, out_shape=[jax.ShapeDtypeStruct(shape, f32) for sh...  54.9 us

profile of v7, /device:TPU:1, one launch (start us, length us, event | category | flops | bytes accessed | tf_op | source)
XLA Modules:
  0.0 56.6 jit_solution(2841722531881386712)
XLA Ops:
  0.6 54.9 %shard_map.189 = (f32[8,64,128]{2,1,0:T(8,128)S(1)}, f32[16,20,128]{2,1,0:T(8,128)S(1)}, f32[8,8,128]{2,1,0:T(8,128)S(1)}, f32[136,64]{1,0:T(8,128)S(1)}) custom-call(bf16[64,8192]{1,0:T(8,128)(2,1)} %bitcast.12, bf16[64,8192]{1,0:T(8,128)(2,1)} %bitcast.13, bf16[128,128]{1,0:T(8,128)(2,1)} %constant.12.clone.refs_0_, f32[2,64,128]{2,1,0:T(8,128)} %constant.13.clone.refs_1_, ...), custom_call_target="tpu_custom_call" | custom-call | tf_op jit(solution)/shard_map/pallas_call | solution.py:506
  55.6 1.0 %shard_map.190 = (f32[512,128]{1,0:T(8,128)}, f32[33,64]{1,0:T(8,128)}, f32[1,64]{1,0:T(1,128)}, f32[64,64]{1,0:T(8,128)}, f32[2,64]{1,0:T(2,128)}, /*index=5*/f32[64,512]{1,0:T(8,128)}, f32[1,512]{1,0:T(1,128)}) custom-call(f32[512,128]{1,0:T(8,128)S(1)} %bitcast.11, f32[16,20,128]{2,1,0:T(8,128)S(1)} %get-tuple-element.19.pieces, ...), custom_call_target="tpu_custom_call" | custom-call | tf_op jit(solution)/shard_map/pallas_call | solution.py:553

commit v8 on v7

--- a/solution.py
+++ b/solution.py
@@ -293,7 +293,8 @@
     sine_first[...] = kept(sine)
     cosine_first[...] = cosine
     pl.semaphore_wait(entered.at[1], 7)
-    greet(entered.at[2])
+    for _, where in dp_peers[:4]:
+        pl.semaphore_signal(entered.at[2], 1, device_id=where, device_id_type=MESH_ID)
     send_inputs((1, 2), (2, 1), (2, 3), (3, 2))
     sine, cosine = sine_cosine(wide(freq_second) * exact_dot(hidden_weight[...], sine))
     sine_second[...] = kept(sine)
@@ -334,7 +335,7 @@
         spectrum[:, :128] += in_real * grad_real + in_imag * grad_imag
         spectrum[:, 128:] += in_real * grad_imag - in_imag * grad_real
 
-    pl.semaphore_wait(entered.at[2], 7)
+    pl.semaphore_wait(entered.at[2], 4)
     send_inputs((2, 2))
     own.wait()
     add_sequence(0)

time: 56.7 us -> 56.7 us (level)
  no operation moved by 1% of the time
where the time goes in v8:
time: 56.7 us; the launch traced here: 56.6 us
  Pallas kernels  56 us (99%)
  between operations  0.64 us (1%)
    pallas_call x1, Pallas kernels, local(): pl.pallas_call(kernel, out_shape=[jax.ShapeDtypeStruct(shape, f32) for sh...  54.9 us

profile of v8, /device:TPU:1, one launch (start us, length us, event | category | flops | bytes accessed | tf_op | source)
XLA Modules:
  0.0 56.6 jit_solution(8360572421400838713)
XLA Ops:
  0.6 54.9 %shard_map.189 = (f32[8,64,128]{2,1,0:T(8,128)S(1)}, f32[16,20,128]{2,1,0:T(8,128)S(1)}, f32[8,8,128]{2,1,0:T(8,128)S(1)}, f32[136,64]{1,0:T(8,128)S(1)}) custom-call(bf16[64,8192]{1,0:T(8,128)(2,1)} %bitcast.12, bf16[64,8192]{1,0:T(8,128)(2,1)} %bitcast.13, bf16[128,128]{1,0:T(8,128)(2,1)} %constant.12.clone.refs_0_, f32[2,64,128]{2,1,0:T(8,128)} %constant.13.clone.refs_1_, ...), custom_call_target="tpu_custom_call" | custom-call | tf_op jit(solution)/shard_map/pallas_call | solution.py:507
  55.6 1.0 %shard_map.190 = (f32[512,128]{1,0:T(8,128)}, f32[33,64]{1,0:T(8,128)}, f32[1,64]{1,0:T(1,128)}, f32[64,64]{1,0:T(8,128)}, f32[2,64]{1,0:T(2,128)}, /*index=5*/f32[64,512]{1,0:T(8,128)}, f32[1,512]{1,0:T(1,128)}) custom-call(f32[512,128]{1,0:T(8,128)S(1)} %bitcast.11, f32[16,20,128]{2,1,0:T(8,128)S(1)} %get-tuple-element.19.pieces, ...), custom_call_target="tpu_custom_call" | custom-call | tf_op jit(solution)/shard_map/pallas_call | solution.py:554
